TPU v7x, 128 devices: a whole 4x4x4 slice. The times are simulated.
128 devices in a mesh: dp: 64 (over z, y_lo, x, core), mp: 2 (over y_hi).
Axes of the slice: x: 4, y: 4 (y_hi: 2, y_lo: 2; y = y_hi * 2 + y_lo), z: 4, core: 2. Of those that a mesh axis runs over, the one named last changes fastest.
Arguments:
- images: bfloat16 [128, 197, 384], P('dp'), may hold values from -6 to 6
- routes: int32 [1, 128, 197, 2], P(None, 'dp'), may hold values from 0 to 3, all different within a row; in each aligned block of 197 rows (0 to 196, 197 to 393, ..., all dimensions but the last counted through in order) at most 104 rows name the same one
- w_qkv: bfloat16 [1, 384, 3, 384], P(None, 'dp', None, 'mp'), may hold values from -0.3125 to 0.3125
- w_proj: bfloat16 [1, 384, 384], P(None, 'mp', 'dp'), may hold values from -2 to 2
- w_in: bfloat16 [1, 4, 384, 1536], P(None, None, 'dp', 'mp'), may hold values from -0.3125 to 0.3125
- w_out: bfloat16 [1, 4, 1536, 384], P(None, None, 'mp', 'dp'), may hold values from -0.3125 to 0.3125
- w_router: bfloat16 [1, 384, 4], P(None, 'dp'), may hold values from -0.625 to 0.625
- ln_gain: bfloat16 [1, 2, 384], P(None, None, 'dp'), may hold values from 0.5 to 1.5
- ln_bias: bfloat16 [1, 2, 384], P(None, None, 'dp'), may hold values from -3 to 3
- cotangent: bfloat16 [128, 197, 384], P('dp'), may hold values from -6 to 6
Outputs:
- activations: float32 [128, 197, 384], P('dp')
- grad_images: float32 [128, 197, 384], P('dp')
- grad_qkv: float32 [1, 384, 3, 384], P(None, 'dp', None, 'mp')
- grad_proj: float32 [1, 384, 384], P(None, 'mp', 'dp')
- grad_in: float32 [1, 4, 384, 1536], P(None, None, 'dp', 'mp')
- grad_out: float32 [1, 4, 1536, 384], P(None, None, 'mp', 'dp')
- grad_router: float32 [1, 384, 4], P(None, 'dp')
- grad_gain: float32 [1, 2, 384], P(None, None, 'dp')
- grad_bias: float32 [1, 2, 384], P(None, None, 'dp')
Inputs may be any that keep to these rules, and one draw needn't show every extreme that they name: `routes`: in each block, each aligned group of 1 images names every expert in at most 104 of its tokens, and some group names some expert in exactly 104; a token's two experts differ.
All inputs are finite; a program needn't handle non-finite values.
Results may differ from a plain program's by a relative error of at most 0.024.
Values may be sent and summed in bfloat16 or wider, within the bound.
A program may use at most 128 MiB of HBM per device.

v0:
```python
import jax
import jax.numpy as jnp
from jax import lax
from jax.sharding import PartitionSpec as P

HD = 64
EXPERTS = 4
TOPK = 2
LAYERS = 1
MICRO = 2
IMG_MB = 1
CAP = 104


EPSILON = 1e-06


def norm_forward(field, gain_row, shift_row):
    mean_value = jnp.mean(field, axis=-1, keepdims=True)
    centered = field - mean_value
    inverse = lax.rsqrt(jnp.mean(centered * centered, axis=-1, keepdims=True) + EPSILON)
    normed = centered * inverse
    return (normed * gain_row + shift_row, normed, inverse)


def norm_backward(grad_out, normed, inverse, gain_row):
    grad_gain = jnp.sum(grad_out * normed, axis=0)
    grad_shift = jnp.sum(grad_out, axis=0)
    scaled = grad_out * gain_row
    grad_in = inverse * (
        scaled
        - jnp.mean(scaled, axis=-1, keepdims=True)
        - normed * jnp.mean(scaled * normed, axis=-1, keepdims=True)
    )
    return (grad_in, grad_gain, grad_shift)


def slot_positions(chosen_ids):
    labels = jnp.arange(EXPERTS, dtype=jnp.int32)
    hit_counts = jnp.sum((chosen_ids[:, :, None] == labels).astype(jnp.int32), axis=1)
    before = jnp.cumsum(hit_counts, axis=0) - hit_counts
    return jnp.take_along_axis(before, chosen_ids, axis=1)


def gelu_slope(inner_pre):
    cumulative = 0.5 * (1.0 + jax.scipy.special.erf(inner_pre * 0.7071067811865476))
    density = jnp.exp(-0.5 * inner_pre * inner_pre) * 0.3989422804014327
    return cumulative + inner_pre * density


def fetch_layer(layer_index, w_qkv, w_proj, w_in, w_out, w_router, ln_gain, ln_bias):
    return (
        lax.all_gather(w_qkv[layer_index], "dp", axis=0, tiled=True),
        lax.all_gather(w_proj[layer_index], "dp", axis=1, tiled=True),
        lax.all_gather(w_in[layer_index], "dp", axis=1, tiled=True),
        lax.all_gather(w_out[layer_index], "dp", axis=2, tiled=True),
        lax.all_gather(w_router[layer_index], "dp", axis=0, tiled=True),
        lax.all_gather(ln_gain[layer_index], "dp", axis=1, tiled=True),
        lax.all_gather(ln_bias[layer_index], "dp", axis=1, tiled=True),
    )


def layer_forward(field, chosen_ids, weights):
    w_qkv, w_proj, w_in, w_out, w_router, ln_gain, ln_bias = weights
    image_count, length, model_width = field.shape
    row_count = image_count * length
    head_count = w_qkv.shape[2] // HD
    score_scale = HD ** (-0.5)
    gain_rows = ln_gain.astype(jnp.float32)
    shift_rows = ln_bias.astype(jnp.float32)
    flat = field.reshape(row_count, model_width)
    first, normed_one, inverse_one = norm_forward(flat, gain_rows[0], shift_rows[0])
    first = first.astype(jnp.bfloat16)
    projected = jnp.einsum("rd,dcf->rcf", first, w_qkv, preferred_element_type=jnp.float32).astype(
        jnp.bfloat16
    )
    projected = projected.reshape(image_count, length, 3, head_count, HD)
    queries = projected[:, :, 0]
    key_rows = projected[:, :, 1]
    value_rows = projected[:, :, 2]
    scores = (
        jnp.einsum("bqhe,bkhe->bhqk", queries, key_rows, preferred_element_type=jnp.float32)
        * score_scale
    )
    log_total = jax.nn.logsumexp(scores, axis=-1)
    attn_weights = jnp.exp(scores - log_total[..., None]).astype(jnp.bfloat16)
    attended = jnp.einsum(
        "bhqk,bkhe->bqhe", attn_weights, value_rows, preferred_element_type=jnp.float32
    )
    attended = attended.astype(jnp.bfloat16).reshape(row_count, head_count * HD)
    partial_attn = jnp.dot(attended, w_proj, preferred_element_type=jnp.float32)
    hidden = flat + lax.psum(partial_attn, "mp")
    second, normed_two, inverse_two = norm_forward(hidden, gain_rows[1], shift_rows[1])
    second = second.astype(jnp.bfloat16)
    logits = jnp.dot(second, w_router, preferred_element_type=jnp.float32)
    router = jax.nn.softmax(logits, axis=-1)
    labels = jnp.arange(EXPERTS, dtype=jnp.int32)
    chosen = (chosen_ids[:, :, None] == labels).astype(jnp.float32)
    gate_values = jnp.sum(router[:, None, :] * chosen, axis=-1)
    slot_index = (chosen_ids * CAP + slot_positions(chosen_ids)).reshape(-1)
    owners = (
        jnp.full((EXPERTS * CAP,), row_count, jnp.int32)
        .at[slot_index]
        .set(jnp.repeat(jnp.arange(row_count, dtype=jnp.int32), TOPK))
    )
    slot_gate = jnp.zeros((EXPERTS * CAP,), jnp.float32).at[slot_index].set(gate_values.reshape(-1))
    padded = jnp.concatenate([second, jnp.zeros((1, model_width), jnp.bfloat16)], axis=0)
    slot_rows = jnp.take(padded, owners, axis=0).reshape(EXPERTS, CAP, model_width)
    inner_pre = jnp.einsum("ecd,edf->ecf", slot_rows, w_in, preferred_element_type=jnp.float32)
    activated = jax.nn.gelu(inner_pre, approximate=False).astype(jnp.bfloat16)
    produced = jnp.einsum("ecf,efd->ecd", activated, w_out, preferred_element_type=jnp.float32)
    produced = produced.reshape(EXPERTS * CAP, model_width)
    picked = jnp.take(produced, slot_index, axis=0).reshape(row_count, TOPK, model_width)
    partial_moe = jnp.sum(gate_values[:, :, None] * picked, axis=1)
    output = hidden + lax.psum(partial_moe.astype(jnp.bfloat16), "mp").astype(jnp.float32)
    record = (
        normed_one,
        inverse_one,
        first,
        projected,
        log_total,
        attended,
        normed_two,
        inverse_two,
        second,
        router,
        chosen,
        slot_index,
        owners,
        slot_gate,
        slot_rows,
        inner_pre,
        activated,
        picked,
    )
    return (output.reshape(image_count, length, model_width), record)


def layer_backward(grad_field, record, weights):
    w_qkv, w_proj, w_in, w_out, w_router, ln_gain, ln_bias = weights
    (
        normed_one,
        inverse_one,
        first,
        projected,
        log_total,
        attended,
        normed_two,
        inverse_two,
        second,
        router,
        chosen,
        slot_index,
        owners,
        slot_gate,
        slot_rows,
        inner_pre,
        activated,
        picked,
    ) = record
    image_count, length, model_width = grad_field.shape
    row_count = image_count * length
    head_count = projected.shape[3]
    score_scale = HD ** (-0.5)
    gain_rows = ln_gain.astype(jnp.float32)
    grad_flat = grad_field.reshape(row_count, model_width)
    padded_grad = jnp.concatenate([grad_flat, jnp.zeros((1, model_width), jnp.float32)], axis=0)
    grad_slots = (jnp.take(padded_grad, owners, axis=0) * slot_gate[:, None]).astype(jnp.bfloat16)
    grad_slots = grad_slots.reshape(EXPERTS, CAP, model_width)
    grad_w_out = jnp.einsum(
        "ecf,ecd->efd", activated, grad_slots, preferred_element_type=jnp.float32
    )
    grad_act = jnp.einsum("ecd,efd->ecf", grad_slots, w_out, preferred_element_type=jnp.float32)
    grad_inner = (grad_act * gelu_slope(inner_pre)).astype(jnp.bfloat16)
    grad_w_in = jnp.einsum(
        "ecd,ecf->edf", slot_rows, grad_inner, preferred_element_type=jnp.float32
    )
    grad_slot_rows = jnp.einsum(
        "ecf,edf->ecd", grad_inner, w_in, preferred_element_type=jnp.float32
    )
    grad_slot_rows = grad_slot_rows.reshape(EXPERTS * CAP, model_width)
    partial_second = jnp.sum(
        jnp.take(grad_slot_rows, slot_index, axis=0).reshape(row_count, TOPK, model_width), axis=1
    )
    partial_gate = jnp.sum(picked * grad_flat[:, None, :], axis=-1)
    grad_second, grad_gate = lax.psum((partial_second, partial_gate), "mp")
    grad_router = jnp.sum(grad_gate[:, :, None] * chosen, axis=1)
    grad_logits = router * (grad_router - jnp.sum(router * grad_router, axis=-1, keepdims=True))
    grad_logits = grad_logits.astype(jnp.bfloat16)
    grad_w_router = jnp.dot(second.T, grad_logits, preferred_element_type=jnp.float32)
    grad_second = grad_second + jnp.dot(grad_logits, w_router.T, preferred_element_type=jnp.float32)
    grad_from_norm, grad_gain_two, grad_shift_two = norm_backward(
        grad_second, normed_two, inverse_two, gain_rows[1]
    )
    grad_hidden = grad_flat + grad_from_norm
    grad_hidden_low = grad_hidden.astype(jnp.bfloat16)
    grad_w_proj = jnp.dot(attended.T, grad_hidden_low, preferred_element_type=jnp.float32)
    grad_attended = jnp.dot(grad_hidden_low, w_proj.T, preferred_element_type=jnp.float32).astype(
        jnp.bfloat16
    )
    grad_attended = grad_attended.reshape(image_count, length, head_count, HD)
    queries = projected[:, :, 0]
    key_rows = projected[:, :, 1]
    value_rows = projected[:, :, 2]
    scores = (
        jnp.einsum("bqhe,bkhe->bhqk", queries, key_rows, preferred_element_type=jnp.float32)
        * score_scale
    )
    probs = jnp.exp(scores - log_total[..., None])
    grad_values = jnp.einsum(
        "bhqk,bqhe->bkhe",
        probs.astype(jnp.bfloat16),
        grad_attended,
        preferred_element_type=jnp.float32,
    )
    grad_probs = jnp.einsum(
        "bqhe,bkhe->bhqk", grad_attended, value_rows, preferred_element_type=jnp.float32
    )
    grad_scores = (
        probs * (grad_probs - jnp.sum(probs * grad_probs, axis=-1, keepdims=True))
    ).astype(jnp.bfloat16)
    grad_queries = (
        jnp.einsum("bhqk,bkhe->bqhe", grad_scores, key_rows, preferred_element_type=jnp.float32)
        * score_scale
    )
    grad_keys = (
        jnp.einsum("bhqk,bqhe->bkhe", grad_scores, queries, preferred_element_type=jnp.float32)
        * score_scale
    )
    grad_projected = jnp.stack([grad_queries, grad_keys, grad_values], axis=2).astype(jnp.bfloat16)
    grad_projected = grad_projected.reshape(row_count, 3, head_count * HD)
    grad_w_qkv = jnp.einsum(
        "rd,rcf->dcf", first, grad_projected, preferred_element_type=jnp.float32
    )
    partial_first = jnp.einsum(
        "rcf,dcf->rd", grad_projected, w_qkv, preferred_element_type=jnp.float32
    )
    grad_first = lax.psum(partial_first.astype(jnp.bfloat16), "mp").astype(jnp.float32)
    grad_input_norm, grad_gain_one, grad_shift_one = norm_backward(
        grad_first, normed_one, inverse_one, gain_rows[0]
    )
    grad_input = grad_hidden + grad_input_norm
    grads = (
        grad_w_qkv,
        grad_w_proj,
        grad_w_in,
        grad_w_out,
        grad_w_router,
        jnp.stack([grad_gain_one, grad_gain_two]),
        jnp.stack([grad_shift_one, grad_shift_two]),
    )
    return (grad_input.reshape(image_count, length, model_width), grads)


def local(images, routes, w_qkv, w_proj, w_in, w_out, w_router, ln_gain, ln_bias, cotangent):
    outputs = []
    grad_parts = []
    totals = []
    for micro_index in range(MICRO):
        start_row = micro_index * IMG_MB
        field = images[start_row : start_row + IMG_MB].astype(jnp.float32)
        fetched = []
        layer_index = 0
        weights = fetch_layer(layer_index, w_qkv, w_proj, w_in, w_out, w_router, ln_gain, ln_bias)
        layer_routes = routes[layer_index, start_row : start_row + IMG_MB].reshape(-1, TOPK)
        field, record = layer_forward(field, layer_routes, weights)
        records = [record]
        fetched.append(weights)
        outputs.append(field)
        grad_field = cotangent[start_row : start_row + IMG_MB].astype(jnp.float32)
        layer_grads = [None] * LAYERS
        for layer_index in reversed(range(LAYERS)):
            weights = fetch_layer(
                layer_index, w_qkv, w_proj, w_in, w_out, w_router, ln_gain, ln_bias
            )
            grad_field, grads = layer_backward(grad_field, records[layer_index], weights)
            layer_grads[layer_index] = grads
        grad_parts.append(grad_field)
        if micro_index == 0:
            totals = layer_grads
        else:
            totals = [
                jax.tree.map(jnp.add, earlier, later) for earlier, later in zip(totals, layer_grads)
            ]
    layer_index = 0
    held = totals[layer_index]
    shards = [
        (
            lax.psum_scatter(held[0], "dp", scatter_dimension=0, tiled=True),
            lax.psum_scatter(held[1], "dp", scatter_dimension=1, tiled=True),
            lax.psum_scatter(held[2], "dp", scatter_dimension=1, tiled=True),
            lax.psum_scatter(held[3], "dp", scatter_dimension=2, tiled=True),
            lax.psum_scatter(held[4], "dp", scatter_dimension=0, tiled=True),
            lax.psum_scatter(held[5], "dp", scatter_dimension=1, tiled=True),
            lax.psum_scatter(held[6], "dp", scatter_dimension=1, tiled=True),
        )
    ]
    return (
        jnp.concatenate(outputs, axis=0),
        jnp.concatenate(grad_parts, axis=0),
        jnp.stack([piece[0] for piece in shards]),
        jnp.stack([piece[1] for piece in shards]),
        jnp.stack([piece[2] for piece in shards]),
        jnp.stack([piece[3] for piece in shards]),
        jnp.stack([piece[4] for piece in shards]),
        jnp.stack([piece[5] for piece in shards]),
        jnp.stack([piece[6] for piece in shards]),
    )


def solution(mesh):
    in_specs = (
        P("dp", None, None),
        P(None, "dp", None, None),
        P(None, "dp", None, "mp"),
        P(None, "mp", "dp"),
        P(None, None, "dp", "mp"),
        P(None, None, "mp", "dp"),
        P(None, "dp", None),
        P(None, None, "dp"),
        P(None, None, "dp"),
        P("dp", None, None),
    )
    out_specs = (
        P("dp", None, None),
        P("dp", None, None),
        P(None, "dp", None, "mp"),
        P(None, "mp", "dp"),
        P(None, None, "dp", "mp"),
        P(None, None, "mp", "dp"),
        P(None, "dp", None),
        P(None, None, "dp"),
        P(None, None, "dp"),
    )
    return jax.shard_map(local, mesh=mesh, in_specs=in_specs, out_specs=out_specs, check_vma=False)
```

profile of v0, /device:TPU:1, one launch (start us, length us, event | category | flops | bytes accessed | tf_op | source)
XLA Modules:
  0.0 1331.0 jit_solution(13719838613397084062)
XLA Ops:
  10.3 85.2 %all-gather.1 = bf16[1,2,384]{1,0,2:T(2,128)(2,1)S(1)} all-gather(bf16[1,2,6]{1,0,2:T(2,128)(2,1)S(1)} %copy.153), channel_id=3, replica_groups=mesh['dp'=64,'mp'=2] {'dp'}, dimensions={2}, use_global_device_ids=true | all-gather | bytes 1560 | tf_op jit(solution)/shard_map/all_gather | solution.py:59
  97.4 77.0 %all-gather = bf16[1,2,384]{1,0,2:T(2,128)(2,1)S(1)} all-gather(bf16[1,2,6]{1,0,2:T(2,128)(2,1)S(1)} %copy.152), channel_id=2, replica_groups=mesh['dp'=64,'mp'=2] {'dp'}, dimensions={2}, use_global_device_ids=true | all-gather | bytes 1560 | tf_op jit(solution)/shard_map/all_gather | solution.py:58
  176.3 78.9 %all-gather.3 = bf16[1,192,384]{1,0,2:T(2,128)(2,1)S(1)} all-gather(bf16[1,192,6]{1,0,2:T(2,128)(2,1)S(1)} %copy.157), channel_id=5, replica_groups=mesh['dp'=64,'mp'=2] {'dp'}, dimensions={2}, use_global_device_ids=true | all-gather | bytes 149760 | tf_op jit(solution)/shard_map/all_gather | solution.py:54
  257.0 78.6 %all-gather.2 = bf16[1,384,3,192]{3,2,0,1:T(4,128)(2,1)S(1)} all-gather(bf16[1,6,3,192]{3,2,0,1:T(4,128)(2,1)S(1)} %bitcast.432), channel_id=4, replica_groups=mesh['dp'=64,'mp'=2] {'dp'}, dimensions={1}, use_global_device_ids=true | all-gather | bytes 449280 | tf_op jit(solution)/shard_map/all_gather | solution.py:53
  344.9 5.9 gather_fusion.3
  354.6 5.9 gather_fusion
  361.7 2.9 scatter_custom_fusion
  364.7 2.9 scatter_custom_fusion.1
  369.6 78.4 %all-gather.4 = bf16[1,384,4]{2,0,1:T(2,128)(2,1)S(1)} all-gather(bf16[1,6,4]{2,0,1:T(2,128)(2,1)S(1)} %copy.161), channel_id=6, replica_groups=mesh['dp'=64,'mp'=2] {'dp'}, dimensions={1}, use_global_device_ids=true | all-gather | bytes 3120 | tf_op jit(solution)/shard_map/all_gather | solution.py:57
  451.2 2.6 gather_fusion.6
  465.2 2.6 fusion.91
  468.9 2.9 fusion.35
  471.8 85.2 %all-gather.12.cloned.1.call-done = bf16[1,4,768,384]{2,1,0,3:T(4,128)(2,1)} async-done(((bf16[1,4,768,6]{2,1,0,3:T(4,128)(2,1)}), bf16[1,4,768,384]{2,1,0,3:T(4,128)(2,1)}) %all-gather.12.cloned.1.call-update) | async-done | bytes 2359312 | tf_op jit(solution)/shard_map/all_gather | solution.py:56
  557.0 5.4 copy.169
  569.2 2.7 fusion.92
  571.9 2.9 fusion.38
  575.4 2.4 gather_fusion.5
  577.7 2.9 multiply_reduce_fusion.1
  582.1 13.3 all-reduce.16
  599.2 3.6 scatter_custom_fusion.2
  603.7 4.1 fusion.30
  607.8 2.9 fusion.176
  610.7 2.3 reshape.558
  614.6 2.5 multiply_reduce_fusion.5
  620.0 3.6 scatter_custom_fusion.3
  624.5 4.1 fusion.27
  629.7 2.6 multiply_reduce_fusion.4
  632.4 4.1 fusion.175
  637.3 2.4 gather_fusion.7
  642.1 2.5 reduce_sum.418
  644.7 2.7 fusion.9
  652.0 2.5 reduce_sum.428
  654.8 5.7 convolution_add_fusion.1
  660.5 31.3 %all-reduce.27.cloned.1.call-done = (f32[197,384]{1,0:T(8,128)}, f32[197,384]{1,0:T(8,128)}) async-done(((f32[197,384]{1,0:T(8,128)}, f32[197,384]{1,0:T(8,128)}), (f32[197,384]{1,0:T(8,128)}, f32[197,384]{1,0:T(8,128)})) %all-reduce.27.cloned.1.call-update) | async-done | bytes 605200 | tf_op jit(solution)/shard_map/psum | solution.py:186
  702.5 3.2 convolution_add_fusion
  705.6 7.5 copy.189
  713.2 5.2 copy.190
  722.4 141.6 %fusion = f32[192,8]{0,1:T(8,128)S(1)} fusion(f32[192,384]{0,1:T(8,128)S(1)} %convolution_add_fusion.3), kind=kCustom, calls=%all-reduce-scatter | all-reduce-scatter fusion | flops 98305 | bytes 301568
  873.7 15.1 %collective-permute-start.9 = (f32[192,8]{0,1:T(8,128)S(1)}, f32[192,8]{0,1:T(8,128)S(1)}, u32[]{:S(2)}, u32[]{:S(2)}) collective-permute-start(f32[192,8]{0,1:T(8,128)S(1)} %fusion), channel_id=1, source_target_pairs={{0,20},{2,22},{4,24},{6,26},{8,28},{10,30},{12,32},{14,34},{16,36}... | collective-permute-start | bytes 18440
  891.5 3.7 collective-permute-start.6
  895.2 2.6 collective-permute-start.5
  897.9 2.4 collective-permute-start.4
  900.4 3.4 collective-permute-start.3
  903.8 3.4 collective-permute-start.2
  907.2 2.2 collective-permute-start.1
  909.5 3.3 collective-permute-start
  920.6 268.9 %all-reduce.14 = (f32[384,4]{0,1:T(4,128)S(1)}, f32[2,384]{1,0:T(2,128)S(1)}, f32[2,384]{1,0:T(2,128)S(1)}) all-reduce(f32[384,4]{0,1:T(4,128)S(1)} %convolution_add_fusion.6, f32[2,384]{1,0:T(2,128)S(1)} %maximum_add_fusion, f32[2,384]{1,0:T(2,128)S(1)} %maximum_add_fusion.1), channel_id=13, replica_groups=mesh['dp'=64,'mp'=2] {'dp'}, use_global_device_ids=true, to_apply=%region_62.67.clone | all-reduce | flops 3072 | bytes 24576
  1191.5 127.4 %all-reduce.25.cloned.1.call-done = (f32[384,3,192]{2,0,1:T(8,128)}, f32[4,384,768]{2,0,1:T(4,128)}, f32[4,768,384]{1,0,2:T(4,128)}) async-done(((f32[384,3,192]{2,0,1:T(8,128)}, f32[4,384,768]{2,0,1:T(4,128)}, f32[4,768,384]{1,0,2:T(4,128)}), (f32[384,3,192]{2,0,1:T(8,128)}, f32[4,384,768]{2,0,1:T(4,128)}, f32[4,768,384]{1,0,2:T(4,128)})) %all-reduce.25.cloned.1.call-update) | async-done | bytes 10321936
  (460 shorter events, 106.3 us)
Async XLA Ops:
  8.0 448.0 %all-reduce.29.cloned.1.call-start = ((), (), s32[]{:S(2)}) async-start(), calls=%async_computation.4 | async-start | bytes 1228800 | tf_op jit(solution)/shard_map/psum | solution.py:92
  95.4 160.4 %copy-start.29 = (bf16[2,197,384]{2,0,1:T(2,128)(2,1)S(1)}, bf16[2,197,384]{2,0,1:T(2,128)(2,1)}, u32[]{:S(2)}) copy-start(bf16[2,197,384]{2,0,1:T(2,128)(2,1)} %param.18) | copy-start | bytes 907780
  97.4 239.6 %copy-start.52 = (f32[384]{0:T(512)}, f32[384]{0:T(512)S(1)}, u32[]{:S(2)}) copy-start(f32[384]{0:T(512)S(1)} %get-tuple-element.77) | copy-start | bytes 4612
  176.3 281.4 %copy-start.54 = (f32[384]{0:T(512)}, f32[384]{0:T(512)S(1)}, u32[]{:S(2)}) copy-start(f32[384]{0:T(512)S(1)} %get-tuple-element.74) | copy-start | bytes 4612
  255.9 84.0 %copy-start.5 = (bf16[1,192,384]{2,1,0:T(8,128)(2,1)}, bf16[1,192,384]{2,1,0:T(8,128)(2,1)S(1)}, u32[]{:S(2)}) copy-start(bf16[1,192,384]{2,1,0:T(8,128)(2,1)S(1)} %copy.158) | copy-start | bytes 442372
  256.4 80.6 %copy-start.58 = (f32[197]{0:T(256)}, f32[197]{0:T(256)S(1)}, u32[]{:S(2)}) copy-start(f32[197]{0:T(256)S(1)} %broadcast_multiply_fusion.11) | copy-start | bytes 2368
  256.7 80.4 %copy-start.66 = (f32[197]{0:T(256)}, f32[197]{0:T(256)S(1)}, u32[]{:S(2)}) copy-start(f32[197]{0:T(256)S(1)} %add_rsqrt_fusion.3) | copy-start | bytes 2368
  256.8 80.1 %copy-start.56 = (f32[197]{0:T(256)}, f32[197]{0:T(256)S(1)}, u32[]{:S(2)}) copy-start(f32[197]{0:T(256)S(1)} %broadcast_multiply_fusion.9) | copy-start | bytes 2368
  257.0 79.9 %copy-start.64 = (f32[197]{0:T(256)}, f32[197]{0:T(256)S(1)}, u32[]{:S(2)}) copy-start(f32[197]{0:T(256)S(1)} %add_rsqrt_fusion.1) | copy-start | bytes 2368
  340.9 124.3 %all-gather.10.cloned.1.call-start = ((), (), s32[]{:S(2)}) async-start(), calls=%async_computation | async-start | bytes 2396160 | tf_op jit(solution)/shard_map/all_gather | solution.py:55
  341.5 215.6 %all-gather.12.cloned.1.call-start = ((), (), s32[]{:S(2)}) async-start(), calls=%async_computation.1 | async-start | bytes 2396160 | tf_op jit(solution)/shard_map/all_gather | solution.py:56
  342.0 349.7 %all-reduce.27.cloned.1.call-start = ((), (), s32[]{:S(2)}) async-start(), calls=%async_computation.3 | async-start | bytes 1228800 | tf_op jit(solution)/shard_map/psum | solution.py:186
  364.6 100.3 %copy-start.96 = (pred[416]{0:T(512)(128)(4,1)}, pred[416]{0:T(512)(128)(4,1)S(1)}, u32[]{:S(2)}) copy-start(pred[416]{0:T(512)(128)(4,1)S(1)} %compare_and_fusion.3) | copy-start | bytes 1252
  367.6 96.5 %copy-start.95 = (pred[416]{0:T(512)(128)(4,1)}, pred[416]{0:T(512)(128)(4,1)S(1)}, u32[]{:S(2)}) copy-start(pred[416]{0:T(512)(128)(4,1)S(1)} %compare_and_fusion.1) | copy-start | bytes 1252
  368.7 79.7 %copy-start.7 = (bf16[1,197,384]{2,0,1:T(2,128)(2,1)}, bf16[1,197,384]{2,0,1:T(2,128)(2,1)S(1)}, u32[]{:S(2)}) copy-start(bf16[1,197,384]{2,0,1:T(2,128)(2,1)S(1)} %get-tuple-element.115) | copy-start | bytes 453892
  456.0 108.6 %copy-start.80 = (s32[1024]{0:T(1024)}, s32[1024]{0:T(1024)S(1)}, u32[]{:S(2)}) copy-start(s32[1024]{0:T(1024)S(1)} %pad_clamp_fusion.2) | copy-start | bytes 12292
  471.8 90.6 %copy-start.1 = (bf16[4,104,768]{2,1,0:T(8,128)(2,1)}, bf16[4,104,768]{2,1,0:T(8,128)(2,1)S(1)}, u32[]{:S(2)}) copy-start(bf16[4,104,768]{2,1,0:T(8,128)(2,1)S(1)} %fusion.35) | copy-start | bytes 1916932
  654.6 260.8 %all-reduce.31.cloned.1.call-start = ((), (), s32[]{:S(2)}) async-start(), calls=%async_computation.5 | async-start | bytes 1228800 | tf_op jit(solution)/shard_map/psum | solution.py:115
  654.7 39.2 %copy-start.87 = (f32[197]{0:T(256)}, f32[197]{0:T(256)S(1)}, u32[]{:S(2)}) copy-start(f32[197]{0:T(256)S(1)} %multiply_reduce_fusion.14) | copy-start | bytes 2368
  654.8 39.1 %copy-start.22 = (bf16[1,197,384]{2,0,1:T(2,128)(2,1)S(1)}, bf16[1,197,384]{2,0,1:T(2,128)(2,1)}, u32[]{:S(2)}) copy-start(bf16[1,197,384]{2,0,1:T(2,128)(2,1)} %copy-done.21) | copy-start | bytes 453892
  654.8 39.1 %copy-start.71 = (f32[197]{0:T(256)S(1)}, f32[197]{0:T(256)}, u32[]{:S(2)}) copy-start(f32[197]{0:T(256)} %copy-done.70) | copy-start | bytes 2368
  702.1 616.7 %all-reduce.25.cloned.1.call-start = ((), (), s32[]{:S(2)}) async-start(), calls=%async_computation.2 | async-start | bytes 21233664
  721.8 150.0 %copy-start.103 = (u32[128]{0:T(128)S(1)}, u32[128]{0:T(128)}, u32[]{:S(2)}) copy-start(u32[128]{0:T(128)} %constant.216) | copy-start | bytes 1540
  721.8 176.0 %copy-start.20 = (bf16[197,384]{1,0:T(8,128)(2,1)S(1)}, bf16[197,384]{1,0:T(8,128)(2,1)}, u32[]{:S(2)}) copy-start(bf16[197,384]{1,0:T(8,128)(2,1)} %copy-done.19) | copy-start | bytes 453892
  721.8 176.0 %copy-start.76 = (f32[197]{0:T(256)S(1)}, f32[197]{0:T(256)}, u32[]{:S(2)}) copy-start(f32[197]{0:T(256)} %copy-done.74) | copy-start | bytes 2368
  721.8 176.0 %copy-start.90 = (f32[197]{0:T(256)S(1)}, f32[197]{0:T(256)}, u32[]{:S(2)}) copy-start(f32[197]{0:T(256)} %copy-done.89) | copy-start | bytes 2368
  721.8 191.0 %copy-start.18 = (bf16[197,384]{1,0:T(8,128)(2,1)S(1)}, bf16[197,384]{1,0:T(8,128)(2,1)}, u32[]{:S(2)}) copy-start(bf16[197,384]{1,0:T(8,128)(2,1)} %copy-done.17) | copy-start | bytes 453892
  721.8 191.0 %copy-start.88 = (f32[197]{0:T(256)S(1)}, f32[197]{0:T(256)}, u32[]{:S(2)}) copy-start(f32[197]{0:T(256)} %copy-done.87) | copy-start | bytes 2368
  721.8 191.2 %copy-start.94 = (f32[384]{0:T(512)S(1)}, f32[384]{0:T(512)}, u32[]{:S(2)}) copy-start(f32[384]{0:T(512)} %get-tuple-element.64) | copy-start | bytes 4612
  721.8 191.2 %copy-start.92 = (f32[384]{0:T(512)S(1)}, f32[384]{0:T(512)}, u32[]{:S(2)}) copy-start(f32[384]{0:T(512)} %get-tuple-element.62) | copy-start | bytes 4612
  721.8 191.2 %copy-start.91 = (f32[384]{0:T(512)S(1)}, f32[384]{0:T(512)}, u32[]{:S(2)}) copy-start(f32[384]{0:T(512)} %get-tuple-element.72) | copy-start | bytes 4612
  721.9 191.2 %copy-start.93 = (f32[384]{0:T(512)S(1)}, f32[384]{0:T(512)}, u32[]{:S(2)}) copy-start(f32[384]{0:T(512)} %get-tuple-element.73) | copy-start | bytes 4612
  864.0 6.5 collective-permute-start.15
  865.3 8.4 collective-permute-start.14
  866.6 22.2 %collective-permute-start.13 = (f32[192,8]{0,1:T(8,128)S(1)}, f32[192,8]{0,1:T(8,128)S(1)}, u32[]{:S(2)}, u32[]{:S(2)}) collective-permute-start(f32[192,8]{0,1:T(8,128)S(1)} %fusion), channel_id=1, source_target_pairs={{0,28},{2,30},{4,32},{6,34},{8,36},{10,38},{12,40},{14,42},{16,44}... | collective-permute-start | bytes 18440
  867.9 22.2 %collective-permute-start.12 = (f32[192,8]{0,1:T(8,128)S(1)}, f32[192,8]{0,1:T(8,128)S(1)}, u32[]{:S(2)}, u32[]{:S(2)}) collective-permute-start(f32[192,8]{0,1:T(8,128)S(1)} %fusion), channel_id=1, source_target_pairs={{0,26},{2,28},{4,30},{6,32},{8,34},{10,36},{12,38},{14,40},{16,42}... | collective-permute-start | bytes 18440
  869.2 22.3 %collective-permute-start.11 = (f32[192,8]{0,1:T(8,128)S(1)}, f32[192,8]{0,1:T(8,128)S(1)}, u32[]{:S(2)}, u32[]{:S(2)}) collective-permute-start(f32[192,8]{0,1:T(8,128)S(1)} %fusion), channel_id=1, source_target_pairs={{0,24},{2,26},{4,28},{6,30},{8,32},{10,34},{12,36},{14,38},{16,40}... | collective-permute-start | bytes 18440
  870.5 24.7 %collective-permute-start.10 = (f32[192,8]{0,1:T(8,128)S(1)}, f32[192,8]{0,1:T(8,128)S(1)}, u32[]{:S(2)}, u32[]{:S(2)}) collective-permute-start(f32[192,8]{0,1:T(8,128)S(1)} %fusion), channel_id=1, source_target_pairs={{0,22},{2,24},{4,26},{6,28},{8,30},{10,32},{12,34},{14,36},{16,38}... | collective-permute-start | bytes 18440
  873.7 24.2 %collective-permute-start.9 = (f32[192,8]{0,1:T(8,128)S(1)}, f32[192,8]{0,1:T(8,128)S(1)}, u32[]{:S(2)}, u32[]{:S(2)}) collective-permute-start(f32[192,8]{0,1:T(8,128)S(1)} %fusion), channel_id=1, source_target_pairs={{0,20},{2,22},{4,24},{6,26},{8,28},{10,30},{12,32},{14,34},{16,36}... | collective-permute-start | bytes 18440
  888.8 11.6 collective-permute-start.8
  890.1 13.7 %collective-permute-start.7 = (f32[192,8]{0,1:T(8,128)S(1)}, f32[192,8]{0,1:T(8,128)S(1)}, u32[]{:S(2)}, u32[]{:S(2)}) collective-permute-start(f32[192,8]{0,1:T(8,128)S(1)} %fusion), channel_id=1, source_target_pairs={{0,16},{2,18},{4,20},{6,22},{8,24},{10,26},{12,28},{14,30},{16,32}... | collective-permute-start | bytes 18440
  891.5 15.7 %collective-permute-start.6 = (f32[192,8]{0,1:T(8,128)S(1)}, f32[192,8]{0,1:T(8,128)S(1)}, u32[]{:S(2)}, u32[]{:S(2)}) collective-permute-start(f32[192,8]{0,1:T(8,128)S(1)} %fusion), channel_id=1, source_target_pairs={{0,14},{2,16},{4,18},{6,20},{8,22},{10,24},{12,26},{14,28},{16,30}... | collective-permute-start | bytes 18440
  895.2 14.3 %collective-permute-start.5 = (f32[192,8]{0,1:T(8,128)S(1)}, f32[192,8]{0,1:T(8,128)S(1)}, u32[]{:S(2)}, u32[]{:S(2)}) collective-permute-start(f32[192,8]{0,1:T(8,128)S(1)} %fusion), channel_id=1, source_target_pairs={{0,12},{2,14},{4,16},{6,18},{8,20},{10,22},{12,24},{14,26},{16,28}... | collective-permute-start | bytes 18440
  897.9 15.1 %collective-permute-start.4 = (f32[192,8]{0,1:T(8,128)S(1)}, f32[192,8]{0,1:T(8,128)S(1)}, u32[]{:S(2)}, u32[]{:S(2)}) collective-permute-start(f32[192,8]{0,1:T(8,128)S(1)} %fusion), channel_id=1, source_target_pairs={{0,10},{2,12},{4,14},{6,16},{8,18},{10,20},{12,22},{14,24},{16,26}... | collective-permute-start | bytes 18440
  900.4 12.7 collective-permute-start.3
  903.8 9.2 collective-permute-start.2
  907.2 5.9 collective-permute-start.1
  909.5 3.8 collective-permute-start
  (80 other events, 491.8 us)
Sparse Core Ops, SparseCore 0:
  341.0 35.5 all-reduce.28
  654.7 37.0 all-reduce.26
  702.3 38.7 all-reduce.30
  743.7 575.1 all-reduce.24
Sparse Core Ops, SparseCore 1:
  343.1 108.6 all-gather.9
  453.3 103.6 all-gather.11
where the time goes:
time: 1340 us; the launch traced here: 1330 us
  blocking collectives  822 us (61%)
  waiting for transfers between devices  245 us (18%)
  local copies, waits for them, and re-layouts  105 us (8%)
  matrix products  51.2 us (4%)
  starting transfers between devices  47.2 us (4%)
  other arithmetic  41.3 us (3%)
  between operations  19.2 us (1%)
    unnamed x2, blocking collectives  411 us
    unnamed x23, waiting for transfers between devices  129 us
    all_gather x1, waiting for transfers between devices, fetch_layer(): lax.all_gather(w_out[layer_index], 'dp', axis=2, tiled=True)  85.2 us
    all_gather x1, blocking collectives, fetch_layer(): lax.all_gather(ln_bias[layer_index], 'dp', axis=1, tiled=True)  85.2 us
    all_gather x1, blocking collectives, fetch_layer(): lax.all_gather(w_proj[layer_index], 'dp', axis=1, tiled=True)  78.9 us
    all_gather x1, blocking collectives, fetch_layer(): lax.all_gather(w_qkv[layer_index], 'dp', axis=0, tiled=True)  78.6 us
    all_gather x1, blocking collectives, fetch_layer(): lax.all_gather(w_router[layer_index], 'dp', axis=0, tiled=True)  78.4 us
    all_gather x1, blocking collectives, fetch_layer(): lax.all_gather(ln_gain[layer_index], 'dp', axis=1, tiled=True)  77 us
  transfers between devices with their start and end apart: 22, of which 4 were waited for; matrix products, arithmetic and copies ran while one was open for 17% of the time, Pallas kernels for 0%

commit v1 on v0

--- a/solution.py
+++ b/solution.py
@@ -6,12 +6,7 @@
 HD = 64
 EXPERTS = 4
 TOPK = 2
-LAYERS = 1
-MICRO = 2
-IMG_MB = 1
 CAP = 104
-
-
 EPSILON = 1e-06
 
 
@@ -37,9 +32,9 @@
 
 def slot_positions(chosen_ids):
     labels = jnp.arange(EXPERTS, dtype=jnp.int32)
-    hit_counts = jnp.sum((chosen_ids[:, :, None] == labels).astype(jnp.int32), axis=1)
-    before = jnp.cumsum(hit_counts, axis=0) - hit_counts
-    return jnp.take_along_axis(before, chosen_ids, axis=1)
+    hit_counts = jnp.sum((chosen_ids[..., None] == labels).astype(jnp.int32), axis=-2)
+    before = jnp.cumsum(hit_counts, axis=1) - hit_counts
+    return jnp.take_along_axis(before, chosen_ids, axis=-1)
 
 
 def gelu_slope(inner_pre):
@@ -48,16 +43,58 @@
     return cumulative + inner_pre * density
 
 
-def fetch_layer(layer_index, w_qkv, w_proj, w_in, w_out, w_router, ln_gain, ln_bias):
-    return (
-        lax.all_gather(w_qkv[layer_index], "dp", axis=0, tiled=True),
-        lax.all_gather(w_proj[layer_index], "dp", axis=1, tiled=True),
-        lax.all_gather(w_in[layer_index], "dp", axis=1, tiled=True),
-        lax.all_gather(w_out[layer_index], "dp", axis=2, tiled=True),
-        lax.all_gather(w_router[layer_index], "dp", axis=0, tiled=True),
-        lax.all_gather(ln_gain[layer_index], "dp", axis=1, tiled=True),
-        lax.all_gather(ln_bias[layer_index], "dp", axis=1, tiled=True),
-    )
+def shard_sizes(w_qkv, w_proj, w_in, w_out, w_router, ln_gain, ln_bias):
+    return [a.size for a in (w_qkv, w_proj, w_in, w_out, w_router, ln_gain, ln_bias)]
+
+
+def gather_weights(w_qkv, w_proj, w_in, w_out, w_router, ln_gain, ln_bias, n):
+    parts = (w_qkv, w_proj, w_in, w_out, w_router, ln_gain, ln_bias)
+    flat = jnp.concatenate([a.reshape(-1) for a in parts])
+    full = lax.all_gather(flat, "dp", axis=0, tiled=True).reshape(n, -1)
+    pieces = []
+    start = 0
+    for a in parts:
+        pieces.append(full[:, start:start + a.size])
+        start += a.size
+    q, p, i, o, r, g, b = pieces
+    _, rq, cq, fq = w_qkv.shape
+    gq = q.reshape(n * rq, cq, fq)
+    _, fp, dp_ = w_proj.shape
+    gp = p.reshape(n, fp, dp_).transpose(1, 0, 2).reshape(fp, n * dp_)
+    _, ei, di, fi = w_in.shape
+    gi = i.reshape(n, ei, di, fi).transpose(1, 0, 2, 3).reshape(ei, n * di, fi)
+    _, eo, fo, do_ = w_out.shape
+    go = o.reshape(n, eo, fo, do_).transpose(1, 2, 0, 3).reshape(eo, fo, n * do_)
+    _, dr, er = w_router.shape
+    gr = r.reshape(n * dr, er)
+    _, two, dg = ln_gain.shape
+    gg = g.reshape(n, two, dg).transpose(1, 0, 2).reshape(two, n * dg)
+    gb = b.reshape(n, two, dg).transpose(1, 0, 2).reshape(two, n * dg)
+    return (gq, gp, gi, go, gr, gg, gb)
+
+
+def scatter_grads(grads, n, shapes):
+    gq, gp, gi, go, gr, gg, gb = grads
+    rows = [
+        gq.reshape(n, -1),
+        gp.reshape(gp.shape[0], n, -1).transpose(1, 0, 2).reshape(n, -1),
+        gi.reshape(gi.shape[0], n, -1, gi.shape[2]).transpose(1, 0, 2, 3).reshape(n, -1),
+        go.reshape(go.shape[0], go.shape[1], n, -1).transpose(2, 0, 1, 3).reshape(n, -1),
+        gr.reshape(n, -1),
+        gg.reshape(gg.shape[0], n, -1).transpose(1, 0, 2).reshape(n, -1),
+        gb.reshape(gb.shape[0], n, -1).transpose(1, 0, 2).reshape(n, -1),
+    ]
+    packed = jnp.concatenate(rows, axis=1)
+    mine = lax.psum_scatter(packed.reshape(-1), "dp", scatter_dimension=0, tiled=True)
+    outs = []
+    start = 0
+    for shape in shapes:
+        size = 1
+        for s in shape:
+            size *= s
+        outs.append(mine[start:start + size].reshape(shape))
+        start += size
+    return outs
 
 
 def layer_forward(field, chosen_ids, weights):
@@ -95,43 +132,32 @@
     logits = jnp.dot(second, w_router, preferred_element_type=jnp.float32)
     router = jax.nn.softmax(logits, axis=-1)
     labels = jnp.arange(EXPERTS, dtype=jnp.int32)
-    chosen = (chosen_ids[:, :, None] == labels).astype(jnp.float32)
+    ids_flat = chosen_ids.reshape(row_count, TOPK)
+    chosen = (ids_flat[:, :, None] == labels).astype(jnp.float32)
     gate_values = jnp.sum(router[:, None, :] * chosen, axis=-1)
-    slot_index = (chosen_ids * CAP + slot_positions(chosen_ids)).reshape(-1)
+    per_image = EXPERTS * CAP
+    image_base = (jnp.arange(image_count, dtype=jnp.int32) * per_image)[:, None, None]
+    slot_index = (chosen_ids * CAP + slot_positions(chosen_ids) + image_base).reshape(-1)
     owners = (
-        jnp.full((EXPERTS * CAP,), row_count, jnp.int32)
+        jnp.full((image_count * per_image,), row_count, jnp.int32)
         .at[slot_index]
         .set(jnp.repeat(jnp.arange(row_count, dtype=jnp.int32), TOPK))
     )
-    slot_gate = jnp.zeros((EXPERTS * CAP,), jnp.float32).at[slot_index].set(gate_values.reshape(-1))
+    slot_gate = (
+        jnp.zeros((image_count * per_image,), jnp.float32).at[slot_index].set(gate_values.reshape(-1))
+    )
     padded = jnp.concatenate([second, jnp.zeros((1, model_width), jnp.bfloat16)], axis=0)
-    slot_rows = jnp.take(padded, owners, axis=0).reshape(EXPERTS, CAP, model_width)
-    inner_pre = jnp.einsum("ecd,edf->ecf", slot_rows, w_in, preferred_element_type=jnp.float32)
+    slot_rows = jnp.take(padded, owners, axis=0).reshape(image_count, EXPERTS, CAP, model_width)
+    inner_pre = jnp.einsum("becd,edf->becf", slot_rows, w_in, preferred_element_type=jnp.float32)
     activated = jax.nn.gelu(inner_pre, approximate=False).astype(jnp.bfloat16)
-    produced = jnp.einsum("ecf,efd->ecd", activated, w_out, preferred_element_type=jnp.float32)
-    produced = produced.reshape(EXPERTS * CAP, model_width)
+    produced = jnp.einsum("becf,efd->becd", activated, w_out, preferred_element_type=jnp.float32)
+    produced = produced.reshape(image_count * per_image, model_width)
     picked = jnp.take(produced, slot_index, axis=0).reshape(row_count, TOPK, model_width)
     partial_moe = jnp.sum(gate_values[:, :, None] * picked, axis=1)
     output = hidden + lax.psum(partial_moe.astype(jnp.bfloat16), "mp").astype(jnp.float32)
     record = (
-        normed_one,
-        inverse_one,
-        first,
-        projected,
-        log_total,
-        attended,
-        normed_two,
-        inverse_two,
-        second,
-        router,
-        chosen,
-        slot_index,
-        owners,
-        slot_gate,
-        slot_rows,
-        inner_pre,
-        activated,
-        picked,
+        normed_one, inverse_one, first, projected, log_total, attended, normed_two, inverse_two,
+        second, router, chosen, slot_index, owners, slot_gate, slot_rows, inner_pre, activated, picked,
     )
     return (output.reshape(image_count, length, model_width), record)
 
@@ -139,24 +165,8 @@
 def layer_backward(grad_field, record, weights):
     w_qkv, w_proj, w_in, w_out, w_router, ln_gain, ln_bias = weights
     (
-        normed_one,
-        inverse_one,
-        first,
-        projected,
-        log_total,
-        attended,
-        normed_two,
-        inverse_two,
-        second,
-        router,
-        chosen,
-        slot_index,
-        owners,
-        slot_gate,
-        slot_rows,
-        inner_pre,
-        activated,
-        picked,
+        normed_one, inverse_one, first, projected, log_total, attended, normed_two, inverse_two,
+        second, router, chosen, slot_index, owners, slot_gate, slot_rows, inner_pre, activated, picked,
     ) = record
     image_count, length, model_width = grad_field.shape
     row_count = image_count * length
@@ -166,19 +176,19 @@
     grad_flat = grad_field.reshape(row_count, model_width)
     padded_grad = jnp.concatenate([grad_flat, jnp.zeros((1, model_width), jnp.float32)], axis=0)
     grad_slots = (jnp.take(padded_grad, owners, axis=0) * slot_gate[:, None]).astype(jnp.bfloat16)
-    grad_slots = grad_slots.reshape(EXPERTS, CAP, model_width)
+    grad_slots = grad_slots.reshape(image_count, EXPERTS, CAP, model_width)
     grad_w_out = jnp.einsum(
-        "ecf,ecd->efd", activated, grad_slots, preferred_element_type=jnp.float32
-    )
-    grad_act = jnp.einsum("ecd,efd->ecf", grad_slots, w_out, preferred_element_type=jnp.float32)
+        "becf,becd->efd", activated, grad_slots, preferred_element_type=jnp.float32
+    )
+    grad_act = jnp.einsum("becd,efd->becf", grad_slots, w_out, preferred_element_type=jnp.float32)
     grad_inner = (grad_act * gelu_slope(inner_pre)).astype(jnp.bfloat16)
     grad_w_in = jnp.einsum(
-        "ecd,ecf->edf", slot_rows, grad_inner, preferred_element_type=jnp.float32
+        "becd,becf->edf", slot_rows, grad_inner, preferred_element_type=jnp.float32
     )
     grad_slot_rows = jnp.einsum(
-        "ecf,edf->ecd", grad_inner, w_in, preferred_element_type=jnp.float32
-    )
-    grad_slot_rows = grad_slot_rows.reshape(EXPERTS * CAP, model_width)
+        "becf,edf->becd", grad_inner, w_in, preferred_element_type=jnp.float32
+    )
+    grad_slot_rows = grad_slot_rows.reshape(image_count * EXPERTS * CAP, model_width)
     partial_second = jnp.sum(
         jnp.take(grad_slot_rows, slot_index, axis=0).reshape(row_count, TOPK, model_width), axis=1
     )
@@ -208,9 +218,7 @@
     )
     probs = jnp.exp(scores - log_total[..., None])
     grad_values = jnp.einsum(
-        "bhqk,bqhe->bkhe",
-        probs.astype(jnp.bfloat16),
-        grad_attended,
+        "bhqk,bqhe->bkhe", probs.astype(jnp.bfloat16), grad_attended,
         preferred_element_type=jnp.float32,
     )
     grad_probs = jnp.einsum(
@@ -252,63 +260,21 @@
     return (grad_input.reshape(image_count, length, model_width), grads)
 
 
-def local(images, routes, w_qkv, w_proj, w_in, w_out, w_router, ln_gain, ln_bias, cotangent):
-    outputs = []
-    grad_parts = []
-    totals = []
-    for micro_index in range(MICRO):
-        start_row = micro_index * IMG_MB
-        field = images[start_row : start_row + IMG_MB].astype(jnp.float32)
-        fetched = []
-        layer_index = 0
-        weights = fetch_layer(layer_index, w_qkv, w_proj, w_in, w_out, w_router, ln_gain, ln_bias)
-        layer_routes = routes[layer_index, start_row : start_row + IMG_MB].reshape(-1, TOPK)
-        field, record = layer_forward(field, layer_routes, weights)
-        records = [record]
-        fetched.append(weights)
-        outputs.append(field)
-        grad_field = cotangent[start_row : start_row + IMG_MB].astype(jnp.float32)
-        layer_grads = [None] * LAYERS
-        for layer_index in reversed(range(LAYERS)):
-            weights = fetch_layer(
-                layer_index, w_qkv, w_proj, w_in, w_out, w_router, ln_gain, ln_bias
-            )
-            grad_field, grads = layer_backward(grad_field, records[layer_index], weights)
-            layer_grads[layer_index] = grads
-        grad_parts.append(grad_field)
-        if micro_index == 0:
-            totals = layer_grads
-        else:
-            totals = [
-                jax.tree.map(jnp.add, earlier, later) for earlier, later in zip(totals, layer_grads)
-            ]
-    layer_index = 0
-    held = totals[layer_index]
-    shards = [
-        (
-            lax.psum_scatter(held[0], "dp", scatter_dimension=0, tiled=True),
-            lax.psum_scatter(held[1], "dp", scatter_dimension=1, tiled=True),
-            lax.psum_scatter(held[2], "dp", scatter_dimension=1, tiled=True),
-            lax.psum_scatter(held[3], "dp", scatter_dimension=2, tiled=True),
-            lax.psum_scatter(held[4], "dp", scatter_dimension=0, tiled=True),
-            lax.psum_scatter(held[5], "dp", scatter_dimension=1, tiled=True),
-            lax.psum_scatter(held[6], "dp", scatter_dimension=1, tiled=True),
-        )
-    ]
-    return (
-        jnp.concatenate(outputs, axis=0),
-        jnp.concatenate(grad_parts, axis=0),
-        jnp.stack([piece[0] for piece in shards]),
-        jnp.stack([piece[1] for piece in shards]),
-        jnp.stack([piece[2] for piece in shards]),
-        jnp.stack([piece[3] for piece in shards]),
-        jnp.stack([piece[4] for piece in shards]),
-        jnp.stack([piece[5] for piece in shards]),
-        jnp.stack([piece[6] for piece in shards]),
-    )
+def make_local(n):
+    def local(images, routes, w_qkv, w_proj, w_in, w_out, w_router, ln_gain, ln_bias, cotangent):
+        shapes = [a.shape for a in (w_qkv, w_proj, w_in, w_out, w_router, ln_gain, ln_bias)]
+        weights = gather_weights(w_qkv, w_proj, w_in, w_out, w_router, ln_gain, ln_bias, n)
+        field = images.astype(jnp.float32)
+        output, record = layer_forward(field, routes[0], weights)
+        grad_input, grads = layer_backward(cotangent.astype(jnp.float32), record, weights)
+        shards = scatter_grads(grads, n, [(1,) + tuple(s[1:]) for s in shapes])
+        return (output, grad_input, *shards)
+
+    return local
 
 
 def solution(mesh):
+    n = mesh.shape["dp"]
     in_specs = (
         P("dp", None, None),
         P(None, "dp", None, None),
@@ -332,4 +298,4 @@
         P(None, None, "dp"),
         P(None, None, "dp"),
     )
-    return jax.shard_map(local, mesh=mesh, in_specs=in_specs, out_specs=out_specs, check_vma=False)
+    return jax.shard_map(make_local(n), mesh=mesh, in_specs=in_specs, out_specs=out_specs, check_vma=False)

time: 1340 us -> 1450 us (1.082)
  waiting for transfers between devices: 245 us -> 1120 us
  blocking collectives: 822 us -> 12.9 us
  local copies, waits for them, and re-layouts: 105 us -> 238 us
  starting transfers between devices: 47.2 us -> 0.21 us
  matrix products: 51.2 us -> 31.6 us
  other arithmetic: 41.3 us -> 22.3 us
    unnamed x23 -> x7, waiting for transfers between devices: 129 us -> 1090 us
    unnamed x2 -> x0, blocking collectives: 411 us -> none
    all_gather x5 -> x0, blocking collectives: 398 us -> none  [the longest x1 85.2 us: fetch_layer(): lax.all_gather(ln_bias[layer_index], 'dp', axis=1, tiled=True)]
    reshape x5 -> x44, local copies, waits for them, and re-layouts: 0.57 us -> 91.1 us  [the longest x2 20.9 us: scatter_grads(): go.reshape(go.shape[0], go.shape[1], n, -1).transpose(2, 0, 1, 3)]
    all_gather x2 -> x0, waiting for transfers between devices: 85.3 us -> none  [the longest x1 85.2 us: fetch_layer(): lax.all_gather(w_out[layer_index], 'dp', axis=2, tiled=True)]
    unnamed x17 -> x2, starting transfers between devices: 46.8 us -> 0.08 us
    psum x1, waiting for transfers between devices: 31.3 us -> 0.01 us  [layer_backward(): grad_second, grad_gate = lax.psum((partial_second, partial_gate), 'mp')]
    psum x1, waiting for transfers between devices: 0.01 us -> 26.3 us  [layer_forward(): lax.psum(partial_moe.astype(jnp.bfloat16), 'mp').astype(jnp.float32)]
  transfers between devices with their start and end apart: 22 -> 5, of which waited for: 4 -> 3; matrix products, arithmetic and copies ran while one was open for 17% -> 11% of each run, Pallas kernels for 0% -> 0%
where the time goes in v1:
time: 1450 us; the launch traced here: 1440 us
  waiting for transfers between devices  1120 us (77%)
  local copies, waits for them, and re-layouts  238 us (16%)
  matrix products  31.6 us (2%)
  other arithmetic  22.3 us (2%)
  between operations  17 us (1%)
    unnamed x7, waiting for transfers between devices  1090 us
    unnamed x145, local copies, waits for them, and re-layouts  32.7 us
  transfers between devices with their start and end apart: 5, of which 3 were waited for; matrix products, arithmetic and copies ran while one was open for 11% of the time, Pallas kernels for 0%

profile of v1, /device:TPU:1, one launch (start us, length us, event | category | flops | bytes accessed | tf_op | source)
XLA Modules:
  0.0 1439.9 jit_solution(15132040750010149788)
XLA Ops:
  16.9 2.7 broadcast.280
  19.6 2.3 dynamic-update-slice
  23.8 2.4 reduce-window.6
  29.8 12.6 gather_fusion.2
  42.5 5.4 scatter_custom_fusion
  50.3 3.0 mul.280
  54.5 3.5 gather_fusion.1
  58.0 522.0 %all-reduce.16.cloned.1.call-done = bf16[2657280]{0:T(1024)(128)(2,1)} async-done(((bf16[2657280]{0:T(1024)(128)(2,1)}), bf16[2657280]{0:T(1024)(128)(2,1)}) %all-reduce.16.cloned.1.call-update) | async-done | bytes 5314576
  580.0 11.8 reshape.498
  600.8 4.9 fusion.82
  607.2 6.3 reshape.507
  613.5 4.3 copy.386
  617.8 5.7 copy.384
  623.5 9.5 reshape.505
  633.0 7.5 copy.385
  640.5 5.4 copy.437
  648.0 3.9 gather_fusion
  651.9 9.3 fusion.2
  663.3 3.8 gather_fusion.3
  667.1 3.0 multiply_reduce_fusion.1
  671.0 12.9 psum.38
  686.8 5.4 scatter_custom_fusion.1
  692.4 4.8 convolution_bitcast_fusion
  697.1 1.7 fusion.8
  701.0 3.4 gather_fusion.4
  705.8 1.8 reshape.519
  707.6 3.6 reduce_sum.209
  712.4 1.6 reshape.528
  714.0 1.7 reshape.513
  715.8 7.1 copy.416
  722.8 2.1 convolution_bitcast_fusion.1
  724.9 3.0 copy.414
  727.9 3.9 copy.415
  731.9 6.1 reshape.525
  738.0 9.2 copy.417
  747.2 12.1 reshape.527
  759.3 8.8 copy.426
  768.1 3.6 multiply_reduce_fusion.2
  771.8 1.7 multiply_reduce_fusion.3
  784.2 1.8 copy.410
  786.0 1.9 reshape.522
  787.9 2.1 constant_dynamic-update-slice_fusion.6
  790.9 5.3 constant_dynamic-update-slice_fusion.4
  796.2 2.5 constant_dynamic-update-slice_fusion.3
  800.5 26.3 %all-reduce.20.cloned.1.call-done = (bf16[394,384]{1,0:T(8,128)(2,1)}, bf16[394,384]{1,0:T(8,128)(2,1)}) async-done(((bf16[394,384]{1,0:T(8,128)(2,1)}, bf16[394,384]{1,0:T(8,128)(2,1)}), (bf16[394,384]{1,0:T(8,128)(2,1)}, bf16[394,384]{1,0:T(8,128)(2,1)})) %all-reduce.20.cloned.1.call-update) | async-done | bytes 605200 | tf_op jit(solution)/shard_map/psum | solution.py:157
  830.4 1.7 dynamic-update-slice.7
  832.1 15.7 %reshape.531 = f32[2657280]{0:T(1024)} reshape(f32[64,41520]{1,0:T(8,128)} %dynamic-update-slice.7) | data formatting | bytes 21258240 | tf_op jit(solution)/shard_map/reshape | solution.py:88
  851.6 570.1 %all-reduce.18.cloned.1.call-done = f32[2657280]{0:T(1024)} async-done(((f32[2657280]{0:T(1024)}), f32[2657280]{0:T(1024)}) %all-reduce.18.cloned.1.call-update) | async-done | bytes 10629136
  (328 shorter events, 71.5 us)
Async XLA Ops:
  7.2 572.8 %all-reduce.16.cloned.1.call-start = ((), (), s32[]{:S(2)}) async-start(), calls=%async_computation.2 | async-start | bytes 10629120
  21.9 4.7 copy-start.15
  22.0 623.9 %all-reduce.12.cloned.1.call-start = ((), (), s32[]{:S(2)}) async-start(), calls=%async_computation | async-start | bytes 1228800 | tf_op jit(solution)/shard_map/psum | solution.py:129
  29.8 18.8 %copy-start.36 = (bf16[2,197,384]{2,0,1:T(2,128)(2,1)S(1)}, bf16[2,197,384]{2,0,1:T(2,128)(2,1)}, u32[]{:S(2)}) copy-start(bf16[2,197,384]{2,0,1:T(2,128)(2,1)} %param.21) | copy-start | bytes 907780
  42.5 6.2 copy-start.55
  48.7 4.6 copy-start.2
  48.8 597.0 %copy-start = (f32[394,384]{1,0:T(8,128)}, f32[394,384]{1,0:T(8,128)S(1)}, u32[]{:S(2)}) copy-start(f32[394,384]{1,0:T(8,128)S(1)} %reshape.490) | copy-start | bytes 1815556
  54.5 3.5 copy-start.42
  591.7 2.3 slice-start
  592.6 2.3 slice-start.1
  593.1 2.5 copy-start.49
  593.3 2.3 copy-start.39
  594.9 4.7 copy-start.25
  600.8 6.3 slice-start.2
  600.8 171.0 %all-reduce.14.cloned.1.call-start = ((), (), s32[]{:S(2)}) async-start(), calls=%async_computation.1 | async-start | bytes 1228800 | tf_op jit(solution)/shard_map/psum | solution.py:196
  607.2 40.4 %copy-start.29 = (bf16[384,4]{1,0:T(8,128)(2,1)}, bf16[384,4]{1,0:T(8,128)(2,1)S(1)}, u32[]{:S(2)}) copy-start(bf16[384,4]{1,0:T(8,128)(2,1)S(1)} %reshape.504) | copy-start | bytes 9220
  648.0 3.9 copy-start.48
  651.9 10.4 copy-start.4
  663.2 3.8 copy-start.54
  667.1 17.8 %copy-start.53 = (s32[394,2]{0,1:T(2,128)S(1)}, s32[394,2]{0,1:T(2,128)}, u32[]{:S(2)}) copy-start(s32[394,2]{0,1:T(2,128)} %eq.30) | copy-start | bytes 9460
  667.1 25.3 %copy-start.8 = (bf16[2,4,104,768]{3,2,0,1:T(8,128)(2,1)S(1)}, bf16[2,4,104,768]{3,2,0,1:T(8,128)(2,1)}, u32[]{:S(2)}) copy-start(bf16[2,4,104,768]{3,2,0,1:T(8,128)(2,1)} %copy-done.7) | copy-start | bytes 3833860
  684.9 26.4 %copy-start.51 = (f32[394]{0:T(512)}, f32[394]{0:T(512)S(1)}, u32[]{:S(2)}) copy-start(f32[394]{0:T(512)S(1)} %multiply_reduce_fusion.8) | copy-start | bytes 4732
  692.3 4.8 copy-start.5
  692.3 4.8 copy-start.9
  692.4 4.8 copy-start.56
  697.1 2.8 copy-start.6
  707.6 6.4 copy-start.14
  711.3 115.5 %all-reduce.20.cloned.1.call-start = ((), (), s32[]{:S(2)}) async-start(), calls=%async_computation.4 | async-start | bytes 1228800 | tf_op jit(solution)/shard_map/psum | solution.py:157
  715.7 7.1 copy-start.13
  759.3 8.8 copy-start.16
  759.3 12.5 copy-start.30
  759.3 12.5 copy-start.47
  759.3 12.5 copy-start.52
  768.1 5.3 copy-start.3
  771.7 2.8 copy-start.26
  773.5 2.5 copy-start.18
  776.4 2.4 copy-start.28
  776.9 2.3 copy-start.31
  776.9 2.7 copy-start.32
  780.4 2.3 copy-start.1
  780.4 2.3 copy-start.40
  780.4 2.3 copy-start.44
  780.4 2.3 copy-start.45
  780.4 2.3 copy-start.50
  790.1 631.6 %all-reduce.18.cloned.1.call-start = ((), (), s32[]{:S(2)}) async-start(), calls=%async_computation.3 | async-start | bytes 21258240
  790.1 6.1 slice-start.3
  790.9 5.3 slice-start.4
  796.2 2.9 copy-start.37
  (19 other events, 24.4 us)
Sparse Core Ops, SparseCore 0:
  22.1 557.8 all-reduce.15
  600.9 37.1 all-reduce.11
  711.4 36.2 all-reduce.13
  790.2 36.5 all-reduce.19
  848.0 573.6 all-reduce.17

commit v2 on v1

--- a/solution.py
+++ b/solution.py
@@ -1,7 +1,14 @@
+import functools
+
 import jax
 import jax.numpy as jnp
 from jax import lax
 from jax.sharding import PartitionSpec as P
+from jax.experimental import pallas as pl
+from jax.experimental.pallas import tpu as pltpu
+
+MESH = pl.DeviceIdType.MESH
+LANES = 128
 
 HD = 64
 EXPERTS = 4
@@ -43,6 +50,68 @@
     return cumulative + inner_pre * density
 
 
+def exchange_kernel(n, gather, x_ref, out_ref, send_sem, recv_sem, local_sem):
+    me = lax.axis_index("dp")
+    mp = lax.axis_index("mp")
+    barrier = pltpu.get_barrier_semaphore()
+
+    def greet(k, carry):
+        peer = lax.rem(me + k, n)
+        pl.semaphore_signal(barrier, inc=1, device_id=(peer, mp), device_id_type=MESH)
+        return carry
+
+    lax.fori_loop(1, n, greet, 0)
+    pl.semaphore_wait(barrier, n - 1)
+    own = pltpu.make_async_copy(x_ref if gather else x_ref.at[me], out_ref.at[me], local_sem)
+    own.start()
+
+    def describe(k):
+        peer = lax.rem(me + k, n)
+        return pltpu.make_async_remote_copy(
+            src_ref=x_ref if gather else x_ref.at[peer],
+            dst_ref=out_ref.at[me],
+            send_sem=send_sem.at[k],
+            recv_sem=recv_sem.at[k],
+            device_id=(peer, mp),
+            device_id_type=MESH,
+        )
+
+    def start(k, carry):
+        describe(k).start()
+        return carry
+
+    def finish(k, carry):
+        describe(k).wait()
+        return carry
+
+    lax.fori_loop(1, n, start, 0)
+    lax.fori_loop(1, n, finish, 0)
+    own.wait()
+
+
+def exchange(x, n, gather, collective_id):
+    rows = x.shape[-2]
+    block_bytes = rows * LANES * x.dtype.itemsize
+    return pl.pallas_call(
+        functools.partial(exchange_kernel, n, gather),
+        out_shape=jax.ShapeDtypeStruct((n, rows, LANES), x.dtype),
+        in_specs=[pl.BlockSpec(memory_space=pl.ANY)],
+        out_specs=pl.BlockSpec(memory_space=pl.ANY),
+        scratch_shapes=[
+            pltpu.SemaphoreType.DMA((n,)),
+            pltpu.SemaphoreType.DMA((n,)),
+            pltpu.SemaphoreType.DMA(()),
+        ],
+        compiler_params=pltpu.CompilerParams(collective_id=collective_id, has_side_effects=True),
+        cost_estimate=pl.CostEstimate(flops=0, bytes_accessed=2 * n * block_bytes, transcendentals=0),
+    )(x)
+
+
+def padded_rows(size, dtype_rows=16):
+    rows = -(-size // LANES)
+    return -(-rows // dtype_rows) * dtype_rows
+
+
 def shard_sizes(w_qkv, w_proj, w_in, w_out, w_router, ln_gain, ln_bias):
     return [a.size for a in (w_qkv, w_proj, w_in, w_out, w_router, ln_gain, ln_bias)]
 
@@ -50,7 +119,10 @@
 def gather_weights(w_qkv, w_proj, w_in, w_out, w_router, ln_gain, ln_bias, n):
     parts = (w_qkv, w_proj, w_in, w_out, w_router, ln_gain, ln_bias)
     flat = jnp.concatenate([a.reshape(-1) for a in parts])
-    full = lax.all_gather(flat, "dp", axis=0, tiled=True).reshape(n, -1)
+    total = flat.shape[0]
+    rows = padded_rows(total)
+    flat = jnp.pad(flat, (0, rows * LANES - total)).reshape(rows, LANES)
+    full = exchange(flat, n, True, 0).reshape(n, rows * LANES)
     pieces = []
     start = 0
     for a in parts:
@@ -85,7 +157,10 @@
         gb.reshape(gb.shape[0], n, -1).transpose(1, 0, 2).reshape(n, -1),
     ]
     packed = jnp.concatenate(rows, axis=1)
-    mine = lax.psum_scatter(packed.reshape(-1), "dp", scatter_dimension=0, tiled=True)
+    total = packed.shape[1]
+    count = padded_rows(total)
+    packed = jnp.pad(packed, ((0, 0), (0, count * LANES - total))).reshape(n, count, LANES)
+    mine = jnp.sum(exchange(packed, n, False, 1), axis=0).reshape(-1)
     outs = []
     start = 0
     for shape in shapes:

time: 1450 us -> 657 us (0.45)
  the two profiles are of different devices: /device:TPU:1 before, /device:TPU:25 now
where the time goes in v2:
time: 657 us; the launch traced here: 647 us
  Pallas kernels  314 us (48%)
  local copies, waits for them, and re-layouts  225 us (34%)
  matrix products  29.5 us (4%)
  other arithmetic  27.4 us (4%)
  waiting for transfers between devices  24.9 us (4%)
  between operations  15.7 us (2%)
  blocking collectives  10.2 us (2%)
    pallas_call x2, Pallas kernels, exchange(): pl.pallas_call(functools.partial(exchange_kernel, n, gather), out_shape=j...  314 us
    unnamed x147, local copies, waits for them, and re-layouts  42.1 us
    psum x1, waiting for transfers between devices, layer_forward(): lax.psum(partial_moe.astype(jnp.bfloat16), 'mp').astype(jnp.float32)  24.8 us
    reshape x2, local copies, waits for them, and re-layouts, scatter_grads(): go.reshape(go.shape[0], go.shape[1], n, -1).transpose(2, 0, 1, 3)  21 us
    reshape x2, local copies, waits for them, and re-layouts, gather_weights(): o.reshape(n, eo, fo, do_).transpose(1, 2, 0, 3).reshape(eo, fo, n * do_)  14.8 us
    slice x9, local copies, waits for them, and re-layouts, scatter_grads(): outs.append(mine[start:start + size].reshape(shape))  13.7 us
  transfers between devices with their start and end apart: 3, of which 1 were waited for; matrix products, arithmetic and copies ran while one was open for 22% of the time, Pallas kernels for 0%

profile of v2, /device:TPU:25, one launch (start us, length us, event | category | flops | bytes accessed | tf_op | source)
XLA Modules:
  0.0 647.3 jit_solution(13975836449964229307)
XLA Ops:
  15.5 105.2 %shard_map.169 = bf16[64,336,128]{2,1,0:T(8,128)(2,1)} custom-call(bf16[336,128]{1,0:T(8,128)(2,1)} %pad_bitcast_fusion.1.x_ref), custom_call_target="tpu_custom_call" | custom-call | bytes 11010048 | tf_op jit(solution)/shard_map/pallas_call | solution.py:95
  120.8 4.0 copy.432
  124.9 2.3 copy-done.2
  137.7 4.9 fusion.80
  142.7 2.4 reduce-window.6
  146.5 12.6 %gather_fusion.2 = s32[788]{0:T(1024)S(1)} fusion(s32[2,197,4]{1,2,0:T(4,128)S(1)} %slice_subtract_fusion, s32[788]{0:T(1024)S(1)} %reshape.561), kind=kCustom, calls=%fused_computation.4 | custom fusion | bytes 15760 | tf_op jit(solution)/shard_map/jit(take_along_axis)/gather | solution.py:44
  159.7 5.3 scatter_custom_fusion
  169.9 1.9 mul.280
  172.4 6.1 reshape.496
  178.5 4.3 copy.309
  182.7 5.7 copy.307
  188.5 9.4 %reshape.494 = bf16[64,4,768,6]{0,3,2,1:T(8,128)(2,1)} reshape(bf16[64,18432]{0,1:T(8,128)(2,1)} %copy.307) | data formatting | bytes 4718592 | tf_op jit(solution)/shard_map/reshape | solution.py:139
  197.9 7.5 %copy.308 = bf16[4,768,64,6]{1,0,3,2:T(4,128)(2,1)} copy(bf16[4,768,64,6]{2,3,1,0:T(8,128)(2,1)} %bitcast.204) | data formatting | bytes 4718592 | tf_op jit(solution)/shard_map/transpose | solution.py:139
  205.4 5.4 copy.360
  210.9 3.4 gather_fusion.1
  217.0 3.5 gather_fusion
  220.5 9.5 %fusion.2 = (bf16[2,4,104,768]{3,2,0,1:T(8,128)(2,1)S(1)}, f32[4,768,2,104]{1,3,2,0:T(8,128)}) fusion(bf16[2,4,104,384]{3,2,1,0:T(8,128)(2,1)S(1)} %bitcast.223, pred[2,4,104]{2,0,1:T(4,128)(4,1)S(1)} %copy.311, bf16[4,384,768,1]{2,0,1,3:T(4,128)(2,1)} %bitcast.216), kind=kOutput, calls=%fused_computation.13 | convolution fusion | flops 532586496 | bytes 6832960 | tf_op jit(solution)/shard_map/becd,edf->becf/dot_general | solution.py:226
  231.1 3.4 gather_fusion.3
  234.5 3.0 multiply_reduce_fusion.1
  237.6 10.2 %psum.38 = f32[394,2]{1,0:T(8,128)S(1)} all-reduce(f32[394,2]{1,0:T(8,128)S(1)} %reduce_sum.220), channel_id=1, replica_groups=mesh['dp'=64,'mp'=2] {'mp'}, use_global_device_ids=true, to_apply=%region_20.22 | all-reduce | flops 788 | bytes 6304 | tf_op jit(solution)/shard_map/psum | solution.py:271
  249.1 5.8 scatter_custom_fusion.1
  255.0 4.8 convolution_bitcast_fusion
  262.6 3.4 gather_fusion.4
  266.0 2.5 broadcast_select_fusion
  268.6 3.0 reshape.508
  271.5 3.5 reduce_sum.218
  276.2 3.1 reshape.502
  279.3 6.9 %copy.339 = f32[4,768,384]{1,0,2:T(4,128)} copy(f32[4,768,384]{2,1,0:T(8,128)} %convolution_bitcast_fusion) | data formatting | bytes 9437184 | tf_op jit(solution)/shard_map/becf,becd->efd/dot_general | solution.py:255
  286.1 2.1 convolution_bitcast_fusion.1
  288.2 3.0 copy.337
  291.3 3.9 copy.338
  295.2 6.1 reshape.514
  301.3 9.2 %copy.340 = f32[64,4,768,6]{0,3,2,1:T(8,128)} copy(f32[64,4,768,6]{2,1,3,0:T(4,128)} %bitcast.213) | data formatting | bytes 9437184 | tf_op jit(solution)/shard_map/transpose | solution.py:154
  310.5 12.1 %reshape.516 = f32[64,18432]{0,1:T(8,128)} reshape(f32[64,4,768,6]{0,3,2,1:T(8,128)} %copy.340) | data formatting | bytes 9437184 | tf_op jit(solution)/shard_map/reshape | solution.py:154
  322.7 8.9 %copy.349 = f32[64,18432]{1,0:T(8,128)} copy(f32[64,18432]{0,1:T(8,128)} %reshape.516) | data formatting | bytes 9437184 | tf_op jit(solution)/shard_map/reshape | solution.py:154
  331.5 2.2 multiply_reduce_fusion.2
  333.8 1.7 multiply_reduce_fusion.3
  335.6 1.8 convert_bitcast_fusion
  350.4 2.0 reshape.511
  354.2 5.3 constant_dynamic-update-slice_fusion.4
  359.6 2.5 constant_dynamic-update-slice_fusion.3
  363.9 24.8 %all-reduce.14.cloned.1.call-done = (bf16[394,384]{1,0:T(8,128)(2,1)}, bf16[394,384]{1,0:T(8,128)(2,1)}) async-done(((bf16[394,384]{1,0:T(8,128)(2,1)}, bf16[394,384]{1,0:T(8,128)(2,1)}), (bf16[394,384]{1,0:T(8,128)(2,1)}, bf16[394,384]{1,0:T(8,128)(2,1)})) %all-reduce.14.cloned.1.call-update) | async-done | bytes 605200 | tf_op jit(solution)/shard_map/psum | solution.py:232
  394.0 4.7 pad_bitcast_fusion
  398.7 6.1 copy.385
  404.9 208.7 %shard_map.170 = f32[64,336,128]{2,1,0:T(8,128)} custom-call(f32[64,336,128]{2,1,0:T(8,128)} %bitcast.203), custom_call_target="tpu_custom_call" | custom-call | bytes 22020096 | tf_op jit(solution)/shard_map/pallas_call | solution.py:95
  613.6 4.7 reduce_sum.232
  618.3 7.7 %slice.115 = f32[3584,2,6]{2,1,0:T(2,128)} reshape(f32[336,128]{1,0:T(8,128)S(1)} %reduce_sum.232) | data formatting | bytes 344064 | tf_op jit(solution)/shard_map/slice | solution.py:170
  625.9 4.8 slice.113
  (324 shorter events, 66.1 us)
Async XLA Ops:
  7.2 207.1 %all-reduce.10.cloned.1.call-start = ((), (), s32[]{:S(2)}) async-start(), calls=%async_computation | async-start | bytes 1228800 | tf_op jit(solution)/shard_map/psum | solution.py:204
  120.8 6.5 copy-start.15
  124.8 2.4 copy-start.2
  128.8 2.5 copy-start.50
  130.6 5.5 copy-start.27
  134.4 3.2 copy-start.39
  134.6 8.1 %copy-start.36 = (f32[2,3,197]{2,1,0:T(4,128)}, f32[2,3,197]{2,1,0:T(4,128)S(1)}, u32[]{:S(2)}) copy-start(f32[2,3,197]{2,1,0:T(4,128)S(1)} %log_add_fusion) | copy-start | bytes 14188
  137.3 196.5 %all-reduce.12.cloned.1.call-start = ((), (), s32[]{:S(2)}) async-start(), calls=%async_computation.1 | async-start | bytes 1228800 | tf_op jit(solution)/shard_map/psum | solution.py:271
  146.5 22.7 %copy-start.35 = (bf16[2,197,384]{2,0,1:T(2,128)(2,1)S(1)}, bf16[2,197,384]{2,0,1:T(2,128)(2,1)}, u32[]{:S(2)}) copy-start(bf16[2,197,384]{2,0,1:T(2,128)(2,1)} %param.21) | copy-start | bytes 907780
  169.2 51.3 %copy-start.48 = (pred[2,4,104]{2,0,1:T(4,128)(4,1)}, pred[2,4,104]{2,0,1:T(4,128)(4,1)S(1)}, u32[]{:S(2)}) copy-start(pred[2,4,104]{2,0,1:T(4,128)(4,1)S(1)} %copy.311) | copy-start | bytes 2500
  172.2 43.6 %copy-start.42 = (f32[384]{0:T(512)}, f32[384]{0:T(512)S(1)}, u32[]{:S(2)}) copy-start(f32[384]{0:T(512)S(1)} %mul.252) | copy-start | bytes 4612
  172.3 43.7 %copy-start.31 = (bf16[384,4]{1,0:T(8,128)(2,1)}, bf16[384,4]{1,0:T(8,128)(2,1)S(1)}, u32[]{:S(2)}) copy-start(bf16[384,4]{1,0:T(8,128)(2,1)S(1)} %reshape.493) | copy-start | bytes 9220
  210.8 23.6 %copy-start.54 = (pred[788]{0:T(1024)(128)(4,1)}, pred[788]{0:T(1024)(128)(4,1)S(1)}, u32[]{:S(2)}) copy-start(pred[788]{0:T(1024)(128)(4,1)S(1)} %get-tuple-element.71) | copy-start | bytes 2368
  216.0 4.4 copy-start.13
  220.5 9.5 %copy-start.18 = (bf16[832,384]{1,0:T(8,128)(2,1)}, bf16[832,384]{1,0:T(8,128)(2,1)S(1)}, u32[]{:S(2)}) copy-start(bf16[832,384]{1,0:T(8,128)(2,1)S(1)} %gather_fusion) | copy-start | bytes 1916932
  220.5 9.5 %copy-start.3 = (bf16[4,768,384,1]{2,1,3,0:T(8,128)(2,1)S(1)}, bf16[4,768,384,1]{2,1,3,0:T(8,128)(2,1)}, u32[]{:S(2)}) copy-start(bf16[4,768,384,1]{2,1,3,0:T(8,128)(2,1)} %copy.360) | copy-start | bytes 7077892
  234.5 20.5 %copy-start.7 = (bf16[2,4,104,768]{3,2,0,1:T(8,128)(2,1)S(1)}, bf16[2,4,104,768]{3,2,0,1:T(8,128)(2,1)}, u32[]{:S(2)}) copy-start(bf16[2,4,104,768]{3,2,0,1:T(8,128)(2,1)} %copy-done.6) | copy-start | bytes 3833860
  248.8 26.4 %copy-start.52 = (f32[394]{0:T(512)}, f32[394]{0:T(512)S(1)}, u32[]{:S(2)}) copy-start(f32[394]{0:T(512)S(1)} %multiply_reduce_fusion.8) | copy-start | bytes 4732
  255.0 4.8 copy-start.4
  255.0 4.8 copy-start.8
  255.0 4.8 copy-start.49
  255.0 4.8 copy-start.57
  262.6 3.4 copy-start.55
  268.5 6.6 %copy-start.14 = (bf16[394,384]{1,0:T(8,128)(2,1)S(1)}, bf16[394,384]{1,0:T(8,128)(2,1)}, u32[]{:S(2)}) copy-start(bf16[394,384]{1,0:T(8,128)(2,1)} %copy-done.13) | copy-start | bytes 907780
  275.1 113.7 %all-reduce.14.cloned.1.call-start = ((), (), s32[]{:S(2)}) async-start(), calls=%async_computation.2 | async-start | bytes 1228800 | tf_op jit(solution)/shard_map/psum | solution.py:232
  279.3 6.9 %copy-start.12 = (bf16[2,4,104,768]{3,2,0,1:T(8,128)(2,1)S(1)}, bf16[2,4,104,768]{3,2,0,1:T(8,128)(2,1)}, u32[]{:S(2)}) copy-start(bf16[2,4,104,768]{3,2,0,1:T(8,128)(2,1)} %copy-done.11) | copy-start | bytes 3833860
  322.6 8.9 %copy-start.16 = (f32[394,2,384]{2,1,0:T(2,128)S(1)}, f32[394,2,384]{2,1,0:T(2,128)}, u32[]{:S(2)}) copy-start(f32[394,2,384]{2,1,0:T(2,128)} %reshape.502) | copy-start | bytes 3631108
  322.6 11.1 %copy-start.43 = (f32[384]{0:T(512)S(1)}, f32[384]{0:T(512)}, u32[]{:S(2)}) copy-start(f32[384]{0:T(512)} %copy-done.42) | copy-start | bytes 4612
  322.6 11.1 %copy-start.47 = (f32[394]{0:T(512)S(1)}, f32[394]{0:T(512)}, u32[]{:S(2)}) copy-start(f32[394]{0:T(512)} %copy-done.46) | copy-start | bytes 4732
  322.6 11.1 %copy-start.53 = (f32[394]{0:T(512)S(1)}, f32[394]{0:T(512)}, u32[]{:S(2)}) copy-start(f32[394]{0:T(512)} %copy-done.52) | copy-start | bytes 4732
  333.8 4.5 copy-start.28
  335.5 3.2 copy-start.1
  335.5 3.2 copy-start.37
  335.5 3.5 copy-start.20
  339.5 2.4 copy-start.30
  340.0 3.3 copy-start.33
  343.9 3.0 copy-start.26
  344.0 2.9 copy-start.32
  344.0 4.2 copy-start.41
  344.0 4.2 copy-start.44
  344.0 4.1 copy-start.45
  344.1 4.1 copy-start.51
  353.5 6.1 slice-start
  354.2 5.3 slice-start.1
  359.6 2.9 copy-start.38
  618.2 12.5 %copy-start.17 = (f32[336,128]{1,0:T(8,128)}, f32[336,128]{1,0:T(8,128)S(1)}, u32[]{:S(2)}) copy-start(f32[336,128]{1,0:T(8,128)S(1)} %reduce_sum.232) | copy-start | bytes 516100
  625.9 4.8 copy-start.34
  632.4 7.3 %slice-start.2 = ((f32[1792,6,4]{2,1,0:T(8,128)}), f32[1,6,4]{2,1,0:T(8,128)S(1)}, s32[]{:S(2)}) async-start(f32[1792,6,4]{2,1,0:T(8,128)} %slice.113), calls=%async_computation.5 | async-start | bytes 8192 | tf_op jit(solution)/shard_map/slice | solution.py:170
  (17 other events, 23.6 us)
Sparse Core Ops, SparseCore 0:
  137.4 33.4 all-reduce.9
  275.2 34.9 all-reduce.11
  353.6 35.0 all-reduce.13

commit v3 on v2

--- a/solution.py
+++ b/solution.py
@@ -160,7 +160,8 @@
     total = packed.shape[1]
     count = padded_rows(total)
     packed = jnp.pad(packed, ((0, 0), (0, count * LANES - total))).reshape(n, count, LANES)
-    mine = jnp.sum(exchange(packed, n, False, 1), axis=0).reshape(-1)
+    received = exchange(packed.astype(jnp.bfloat16), n, False, 1)
+    mine = jnp.sum(received.astype(jnp.float32), axis=0).reshape(-1)
     outs = []
     start = 0
     for shape in shapes:

time: 657 us -> 554 us (0.84)
  the two profiles are of different devices: /device:TPU:25 before, /device:TPU:1 now
where the time goes in v3:
time: 554 us; the launch traced here: 544 us
  local copies, waits for them, and re-layouts  219 us (40%)
  Pallas kernels  204 us (37%)
  waiting for transfers between devices  30.1 us (5%)
  other arithmetic  29.8 us (5%)
  matrix products  29.4 us (5%)
  between operations  15.6 us (3%)
  blocking collectives  15 us (3%)
    pallas_call x2, Pallas kernels, exchange(): pl.pallas_call(functools.partial(exchange_kernel, n, gather), out_shape=j...  204 us
    unnamed x147, local copies, waits for them, and re-layouts  33.4 us
    psum x1, waiting for transfers between devices, layer_forward(): lax.psum(partial_moe.astype(jnp.bfloat16), 'mp').astype(jnp.float32)  30.1 us
    reshape x2, local copies, waits for them, and re-layouts, scatter_grads(): go.reshape(go.shape[0], go.shape[1], n, -1).transpose(2, 0, 1, 3)  15.6 us
    psum x1, blocking collectives, layer_backward(): grad_second, grad_gate = lax.psum((partial_second, partial_gate), 'mp')  15 us
    reshape x2, local copies, waits for them, and re-layouts, gather_weights(): o.reshape(n, eo, fo, do_).transpose(1, 2, 0, 3).reshape(eo, fo, n * do_)  14.9 us
    gather x1, local copies, waits for them, and re-layouts, layer_forward(): jnp.take(produced, slot_index, axis=0).reshape(row_count, TOPK, model_width)  14.8 us
    slice x9, local copies, waits for them, and re-layouts, scatter_grads(): outs.append(mine[start:start + size].reshape(shape))  13.7 us
  transfers between devices with their start and end apart: 3, of which 1 were waited for; matrix products, arithmetic and copies ran while one was open for 24% of the time, Pallas kernels for 0%

profile of v3, /device:TPU:1, one launch (start us, length us, event | category | flops | bytes accessed | tf_op | source)
XLA Modules:
  0.0 543.6 jit_solution(18043408648978278987)
XLA Ops:
  15.6 102.2 %shard_map.169 = bf16[64,336,128]{2,1,0:T(8,128)(2,1)} custom-call(bf16[336,128]{1,0:T(8,128)(2,1)} %pad_bitcast_fusion.1.x_ref), custom_call_target="tpu_custom_call" | custom-call | bytes 11010048 | tf_op jit(solution)/shard_map/pallas_call | solution.py:95
  117.8 4.0 copy.429
  122.0 2.2 copy-done
  134.7 4.9 fusion.81
  139.6 2.4 reduce-window.6
  143.4 12.6 %gather_fusion.2 = s32[788]{0:T(1024)S(1)} fusion(s32[2,197,4]{1,2,0:T(4,128)S(1)} %slice_subtract_fusion, s32[788]{0:T(1024)S(1)} %reshape.572), kind=kCustom, calls=%fused_computation.4 | custom fusion | bytes 15760 | tf_op jit(solution)/shard_map/jit(take_along_axis)/gather | solution.py:44
  156.0 5.3 scatter_custom_fusion
  164.2 6.1 %reshape.508 = bf16[64,4,6,768]{3,2,1,0:T(8,128)(2,1)} reshape(bf16[64,18432]{1,0:T(8,128)(2,1)} %get-tuple-element.74) | data formatting | bytes 4718592 | tf_op jit(solution)/shard_map/reshape | solution.py:137
  170.3 4.3 copy.309
  174.5 5.7 %copy.307 = bf16[64,18432]{0,1:T(8,128)(2,1)} copy(bf16[64,18432]{1,0:T(8,128)(2,1)} %get-tuple-element.75) | data formatting | bytes 4718592 | tf_op jit(solution)/shard_map/slice | solution.py:129
  180.3 9.4 %reshape.506 = bf16[64,4,768,6]{0,3,2,1:T(8,128)(2,1)} reshape(bf16[64,18432]{0,1:T(8,128)(2,1)} %copy.307) | data formatting | bytes 4718592 | tf_op jit(solution)/shard_map/reshape | solution.py:139
  189.7 7.5 %copy.308 = bf16[4,768,64,6]{1,0,3,2:T(4,128)(2,1)} copy(bf16[4,768,64,6]{2,3,1,0:T(8,128)(2,1)} %bitcast.202) | data formatting | bytes 4718592 | tf_op jit(solution)/shard_map/transpose | solution.py:139
  197.2 5.4 copy.360
  204.2 3.1 mul.280
  209.9 3.4 gather_fusion.1
  216.5 3.5 gather_fusion
  220.0 9.5 %fusion.2 = (bf16[2,4,104,768]{3,2,0,1:T(8,128)(2,1)S(1)}, f32[4,768,2,104]{1,3,2,0:T(8,128)}) fusion(bf16[2,4,104,384]{3,2,1,0:T(8,128)(2,1)S(1)} %bitcast.219, pred[2,4,104]{2,0,1:T(4,128)(4,1)S(1)} %copy.311, bf16[4,384,768,1]{2,0,1,3:T(4,128)(2,1)} %bitcast.211), kind=kOutput, calls=%fused_computation.16 | convolution fusion | flops 532586496 | bytes 6832960 | tf_op jit(solution)/shard_map/becd,edf->becf/dot_general | solution.py:227
  230.6 14.8 %gather_fusion.3 = f32[788,384]{1,0:T(8,128)} fusion(f32[832,384]{1,0:T(8,128)S(1)} %bitcast.200, s32[1024]{0:T(1024)S(1)} %get-tuple-element.98), kind=kCustom, calls=%fused_computation.clone | custom fusion | bytes 2423888 | tf_op jit(solution)/shard_map/jit(_take)/gather | solution.py:231
  245.4 3.1 multiply_reduce_fusion.1
  249.3 15.0 %psum.38 = f32[394,2]{1,0:T(8,128)} all-reduce(f32[394,2]{1,0:T(8,128)} %reduce_sum.220), channel_id=1, replica_groups=mesh['dp'=64,'mp'=2] {'mp'}, use_global_device_ids=true, to_apply=%region_20.22 | all-reduce | flops 788 | bytes 6304 | tf_op jit(solution)/shard_map/psum | solution.py:272
  264.4 1.6 copy.323
  270.1 1.7 reshape.590
  271.8 6.0 %scatter_custom_fusion.1 = f32[832]{0:T(1024)} fusion(s32[788]{0:T(1024)} %copy-done.59, f32[788]{0:T(1024)} %reshape.590, f32[]{:T(128)} %constant.56.clone.1), kind=kCustom, calls=%fused_computation.164 | custom fusion | bytes 3840 | tf_op jit(solution)/shard_map/scatter | solution.py:223
  280.0 4.2 bitcast_convert_fusion
  284.2 3.1 fusion.8
  288.4 3.7 gather_fusion.4
  293.6 1.8 reshape.520
  295.4 3.7 reduce_sum.218
  299.3 1.8 reshape.514
  302.0 5.0 copy.339
  306.9 7.7 %copy.340 = bf16[64,4,768,6]{0,3,2,1:T(8,128)(2,1)} copy(bf16[64,4,768,6]{2,1,3,0:T(4,128)(2,1)} %bitcast.214) | data formatting | bytes 4718592 | tf_op jit(solution)/shard_map/transpose | solution.py:154
  314.6 9.5 %reshape.528 = bf16[64,18432]{0,1:T(8,128)(2,1)} reshape(bf16[64,4,768,6]{0,3,2,1:T(8,128)(2,1)} %copy.340) | data formatting | bytes 4718592 | tf_op jit(solution)/shard_map/reshape | solution.py:154
  324.2 6.1 %copy.349 = bf16[64,18432]{1,0:T(8,128)(2,1)} copy(bf16[64,18432]{0,1:T(8,128)(2,1)} %reshape.528) | data formatting | bytes 4718592 | tf_op jit(solution)/shard_map/reshape | solution.py:154
  330.3 2.1 bitcast_convert_fusion.1
  332.3 1.8 copy.337
  334.2 2.5 copy.338
  336.7 5.7 %reshape.526 = bf16[64,18432]{1,0:T(8,128)(2,1)} reshape(bf16[64,4,6,768]{3,2,1,0:T(8,128)(2,1)} %copy.338) | data formatting | bytes 4718592 | tf_op jit(solution)/shard_map/reshape | solution.py:153
  342.4 3.6 multiply_reduce_fusion.2
  346.1 2.2 multiply_reduce_fusion.3
  359.3 3.3 constant_dynamic-update-slice_fusion.4
  366.1 30.1 %all-reduce.14.cloned.1.call-done = (bf16[394,384]{1,0:T(8,128)(2,1)}, bf16[394,384]{1,0:T(8,128)(2,1)}) async-done(((bf16[394,384]{1,0:T(8,128)(2,1)}, bf16[394,384]{1,0:T(8,128)(2,1)}), (bf16[394,384]{1,0:T(8,128)(2,1)}, bf16[394,384]{1,0:T(8,128)(2,1)})) %all-reduce.14.cloned.1.call-update) | async-done | bytes 605200 | tf_op jit(solution)/shard_map/psum | solution.py:233
  402.3 2.9 pad_bitcast_fusion
  405.2 3.3 copy.382
  408.5 101.7 %shard_map.170 = bf16[64,336,128]{2,1,0:T(8,128)(2,1)} custom-call(bf16[64,336,128]{2,1,0:T(8,128)(2,1)} %bitcast.204), custom_call_target="tpu_custom_call" | custom-call | bytes 11010048 | tf_op jit(solution)/shard_map/pallas_call | solution.py:95
  510.2 3.4 convert_reduce_fusion
  513.5 4.8 slice.113
  518.3 7.7 %slice.115 = f32[3584,2,6]{2,1,0:T(2,128)} reshape(f32[336,128]{1,0:T(8,128)S(1)} %convert_reduce_fusion) | data formatting | bytes 344064 | tf_op jit(solution)/shard_map/slice | solution.py:171
  527.9 1.6 reshape.535
  (326 shorter events, 71.2 us)
Async XLA Ops:
  7.2 206.2 %all-reduce.10.cloned.1.call-start = ((), (), s32[]{:S(2)}) async-start(), calls=%async_computation | async-start | bytes 1228800 | tf_op jit(solution)/shard_map/psum | solution.py:205
  117.8 7.8 %copy-start.16 = (bf16[2,197,384]{2,0,1:T(2,128)(2,1)S(1)}, bf16[2,197,384]{2,0,1:T(2,128)(2,1)}, u32[]{:S(2)}) copy-start(bf16[2,197,384]{2,0,1:T(2,128)(2,1)} %param.12) | copy-start | bytes 907780
  121.9 2.4 copy-start
  125.3 3.8 copy-start.42
  125.7 3.4 copy-start.55
  131.7 2.8 copy-start.36
  133.0 6.6 %copy-start.29 = (bf16[192,384]{0,1:T(8,128)(2,1)}, bf16[192,384]{0,1:T(8,128)(2,1)S(1)}, u32[]{:S(2)}) copy-start(bf16[192,384]{0,1:T(8,128)(2,1)S(1)} %reshape.504) | copy-start | bytes 442372
  134.2 211.9 %all-reduce.12.cloned.1.call-start = ((), (), s32[]{:S(2)}) async-start(), calls=%async_computation.1 | async-start | bytes 1228800 | tf_op jit(solution)/shard_map/psum | solution.py:272
  156.0 7.9 %copy-start.59 = (s32[788]{0:T(1024)}, s32[788]{0:T(1024)S(1)}, u32[]{:S(2)}) copy-start(s32[788]{0:T(1024)S(1)} %fusion.70) | copy-start | bytes 9460
  163.4 49.9 %copy-start.1 = (f32[394,384]{1,0:T(8,128)}, f32[394,384]{1,0:T(8,128)S(1)}, u32[]{:S(2)}) copy-start(f32[394,384]{1,0:T(8,128)S(1)} %reshape.490) | copy-start | bytes 1815556
  163.7 51.2 %copy-start.45 = (f32[384]{0:T(512)}, f32[384]{0:T(512)S(1)}, u32[]{:S(2)}) copy-start(f32[384]{0:T(512)S(1)} %mul.252) | copy-start | bytes 4612
  164.2 55.9 %copy-start.51 = (pred[2,4,104]{2,0,1:T(4,128)(4,1)}, pred[2,4,104]{2,0,1:T(4,128)(4,1)S(1)}, u32[]{:S(2)}) copy-start(pred[2,4,104]{2,0,1:T(4,128)(4,1)S(1)} %copy.311) | copy-start | bytes 2500
  197.2 5.4 copy-start.33
  202.7 5.3 copy-start.3
  209.9 20.7 %copy-start.44 = (s32[1024]{0:T(1024)}, s32[1024]{0:T(1024)S(1)}, u32[]{:S(2)}) copy-start(s32[1024]{0:T(1024)S(1)} %get-tuple-element.98) | copy-start | bytes 12292
  215.9 4.2 copy-start.39
  220.0 9.5 %copy-start.17 = (bf16[832,384]{1,0:T(8,128)(2,1)}, bf16[832,384]{1,0:T(8,128)(2,1)S(1)}, u32[]{:S(2)}) copy-start(bf16[832,384]{1,0:T(8,128)(2,1)S(1)} %gather_fusion) | copy-start | bytes 1916932
  220.0 9.5 %copy-start.6 = (bf16[4,768,384,1]{2,1,3,0:T(8,128)(2,1)S(1)}, bf16[4,768,384,1]{2,1,3,0:T(8,128)(2,1)}, u32[]{:S(2)}) copy-start(bf16[4,768,384,1]{2,1,3,0:T(8,128)(2,1)} %copy.360) | copy-start | bytes 7077892
  245.4 34.6 %copy-start.13 = (bf16[2,4,104,768]{3,2,0,1:T(8,128)(2,1)S(1)}, bf16[2,4,104,768]{3,2,0,1:T(8,128)(2,1)}, u32[]{:S(2)}) copy-start(bf16[2,4,104,768]{3,2,0,1:T(8,128)(2,1)} %copy-done.12) | copy-start | bytes 3833860
  279.1 5.0 copy-start.7
  279.1 5.0 copy-start.14
  284.2 3.2 copy-start.8
  293.6 5.5 %copy-start.40 = (f32[394]{0:T(512)S(1)}, f32[394]{0:T(512)}, u32[]{:S(2)}) copy-start(f32[394]{0:T(512)} %copy-done.39) | copy-start | bytes 4732
  293.6 5.5 %copy-start.53 = (f32[394]{0:T(512)S(1)}, f32[394]{0:T(512)}, u32[]{:S(2)}) copy-start(f32[394]{0:T(512)} %multiply_reduce_fusion.8) | copy-start | bytes 4732
  295.4 3.9 copy-start.15
  299.1 97.1 %all-reduce.14.cloned.1.call-start = ((), (), s32[]{:S(2)}) async-start(), calls=%async_computation.2 | async-start | bytes 1228800 | tf_op jit(solution)/shard_map/psum | solution.py:233
  324.2 6.1 %copy-start.10 = (bf16[2,4,104,768]{3,2,0,1:T(8,128)(2,1)S(1)}, bf16[2,4,104,768]{3,2,0,1:T(8,128)(2,1)}, u32[]{:S(2)}) copy-start(bf16[2,4,104,768]{3,2,0,1:T(8,128)(2,1)} %copy-done.9) | copy-start | bytes 3833860
  324.2 6.1 %copy-start.52 = (pred[2,4,104]{2,0,1:T(4,128)(4,1)S(1)}, pred[2,4,104]{2,0,1:T(4,128)(4,1)}, u32[]{:S(2)}) copy-start(pred[2,4,104]{2,0,1:T(4,128)(4,1)} %copy-done.51) | copy-start | bytes 2500
  336.6 5.8 %copy-start.20 = (f32[394,2]{1,0:T(8,128)S(1)}, f32[394,2]{1,0:T(8,128)}, u32[]{:S(2)}) copy-start(f32[394,2]{1,0:T(8,128)} %copy.302) | copy-start | bytes 9460
  336.6 9.4 %copy-start.38 = (f32[394]{0:T(512)S(1)}, f32[394]{0:T(512)}, u32[]{:S(2)}) copy-start(f32[394]{0:T(512)} %copy-done.37) | copy-start | bytes 4732
  336.6 9.4 %copy-start.41 = (f32[394]{0:T(512)S(1)}, f32[394]{0:T(512)}, u32[]{:S(2)}) copy-start(f32[394]{0:T(512)} %copy-done.39) | copy-start | bytes 4732
  336.6 9.4 %copy-start.46 = (f32[384]{0:T(512)S(1)}, f32[384]{0:T(512)}, u32[]{:S(2)}) copy-start(f32[384]{0:T(512)} %copy-done.45) | copy-start | bytes 4612
  336.6 9.4 %copy-start.48 = (f32[394]{0:T(512)S(1)}, f32[394]{0:T(512)}, u32[]{:S(2)}) copy-start(f32[394]{0:T(512)} %copy-done.47) | copy-start | bytes 4732
  336.7 9.4 %copy-start.54 = (f32[394]{0:T(512)S(1)}, f32[394]{0:T(512)}, u32[]{:S(2)}) copy-start(f32[394]{0:T(512)} %multiply_reduce_fusion.8) | copy-start | bytes 4732
  342.4 5.9 %copy-start.4 = (f32[394,384]{1,0:T(8,128)S(1)}, f32[394,384]{1,0:T(8,128)}, u32[]{:S(2)}) copy-start(f32[394,384]{1,0:T(8,128)} %copy-done.3) | copy-start | bytes 1815556
  346.0 3.5 copy-start.30
  353.1 2.5 copy-start.2
  353.1 2.5 copy-start.43
  353.1 2.5 copy-start.49
  353.1 2.5 copy-start.50
  353.1 2.5 copy-start.56
  358.6 4.0 copy-start.5
  362.6 2.1 copy-start.35
  513.5 12.5 %copy-start.19 = (f32[336,128]{1,0:T(8,128)}, f32[336,128]{1,0:T(8,128)S(1)}, u32[]{:S(2)}) copy-start(f32[336,128]{1,0:T(8,128)S(1)} %convert_reduce_fusion) | copy-start | bytes 516100
  518.3 7.7 %slice-start = ((f32[1792,6,4]{2,1,0:T(8,128)}), f32[1,6,4]{2,1,0:T(8,128)S(1)}, s32[]{:S(2)}) async-start(f32[1792,6,4]{2,1,0:T(8,128)} %slice.113), calls=%async_computation.3 | async-start | bytes 8192 | tf_op jit(solution)/shard_map/slice | solution.py:171
  526.0 6.9 %copy-start.18 = (bf16[394,384]{1,0:T(8,128)(2,1)S(1)}, bf16[394,384]{1,0:T(8,128)(2,1)}, u32[]{:S(2)}) copy-start(bf16[394,384]{1,0:T(8,128)(2,1)} %get-tuple-element.65) | copy-start | bytes 907780
  526.0 6.1 %slice-start.1 = ((f32[336,128]{1,0:T(8,128)}), f32[27,128]{1,0:T(8,128)S(1)}, s32[]{:S(2)}) async-start(f32[336,128]{1,0:T(8,128)} %copy-done.19), calls=%async_computation.4 | async-start | bytes 32768 | tf_op jit(solution)/shard_map/slice | solution.py:171
  530.7 4.8 copy-start.32
  (17 other events, 20.3 us)
Sparse Core Ops, SparseCore 0:
  134.3 38.9 all-reduce.9
  299.2 37.1 all-reduce.11
  358.7 37.3 all-reduce.13
